TPU v7x, 32 devices: a whole 2x2x4 slice. The times are simulated.
32 devices in a mesh: batch: 4 (over y, core), seq: 8 (over z, x).
Axes of the slice: x: 2, y: 2, z: 4, core: 2. Of those that a mesh axis runs over, the one named last changes fastest.
Arguments:
- tokens: bfloat16 [4, 1024, 1024], P('batch', 'seq'), may hold values from -6 to 6
- w_query: bfloat16 [512, 512], replicated, may hold values from -0.25 to 0.25
- w_value: bfloat16 [512, 512], replicated, may hold values from -0.25 to 0.25
- w_out: bfloat16 [512, 512], replicated, may hold values from -0.25 to 0.25
- long_filter: float32 [512, 1024], P('seq'), may hold values from -0.1875 to 0.1875
- cotangent: bfloat16 [4, 1024, 1024], P('batch', 'seq'), may hold values from -6 to 6
Outputs:
- block_out: bfloat16 [4, 1024, 1024], P('batch', 'seq')
- grad_tokens: bfloat16 [4, 1024, 1024], P('batch', 'seq')
- grad_query: float32 [512, 512], P('seq')
- grad_value: float32 [512, 512], P('seq')
- grad_out: float32 [512, 512], P('seq')
- grad_filter: float32 [512, 1024], P('seq')
All inputs are finite; a program needn't handle non-finite values.
Results may differ from a plain program's by a relative error of at most 0.017.
Values may be sent and summed in bfloat16 or wider, within the bound.
A program may use at most 64 MiB of HBM per device.

v0:
```python
import functools
import math

import jax
import jax.numpy as jnp
import numpy as np
from jax import lax
from jax.experimental import pallas as pl
from jax.experimental.pallas import tpu as pltpu
from jax.sharding import PartitionSpec as P

precise = lax.Precision.HIGH


def swapped(x, axis, stride):
    return lax.ppermute(x, axis, [(i, i ^ 1 << stride) for i in range(lax.axis_size(axis))])


def angle_tables(count_rows, count_cols, period):
    left = lax.broadcasted_iota(jnp.int32, (count_rows, count_cols), 0)
    right = lax.broadcasted_iota(jnp.int32, (count_rows, count_cols), 1)
    turns = left * right % period
    angle = turns.astype(jnp.float32) * (2.0 * math.pi / period)
    return (jnp.cos(angle), jnp.sin(angle))


def rotation(cosines, sines, direction):
    upper = jnp.stack([cosines, direction * sines])
    lower_row = jnp.stack([-direction * sines, cosines])
    return jnp.stack([upper, lower_row])


def split_sizes(length):
    period = 2 * length
    first = 1 << (period.bit_length() - 1 + 1) // 2
    return (first, period // first)


def make_tables(first, second):
    cos_first, sin_first = angle_tables(first, first, first)
    cos_twist, sin_twist = angle_tables(first, second, first * second)
    cos_second, sin_second = angle_tables(second, second, second)
    forward_first = rotation(cos_first, sin_first, 1.0)
    inverse_first = rotation(cos_first, sin_first, -1.0)
    forward_second = rotation(cos_second, sin_second, 1.0)
    inverse_second = rotation(cos_second, sin_second, -1.0)
    return (forward_first, inverse_first, forward_second, inverse_second, cos_twist, sin_twist)


def forward_spectrum(signal, tables, first, second):
    forward_first, inverse_first, forward_second, inverse_second, cos_twist, sin_twist = tables
    lower = first // 2
    folded = signal.reshape(2, signal.shape[1], lower, second)
    section = jnp.einsum("brnm,abnk->arkm", folded, forward_first[:, :, :lower], precision=precise)
    turned = jnp.stack(
        [
            section[0] * cos_twist + section[1] * sin_twist,
            section[1] * cos_twist - section[0] * sin_twist,
        ]
    )
    return jnp.einsum("brkm,abmj->arkj", turned, forward_second, precision=precise)


def inverse_spectrum(spectrum, tables, first, second, both):
    forward_first, inverse_first, forward_second, inverse_second, cos_twist, sin_twist = tables
    lower = first // 2
    rows = spectrum.shape[1]
    inner = jnp.einsum("brkj,abjm->arkm", spectrum, inverse_second, precision=precise)
    turned = jnp.stack(
        [inner[0] * cos_twist - inner[1] * sin_twist, inner[1] * cos_twist + inner[0] * sin_twist]
    )
    if both:
        signal = jnp.einsum(
            "brkm,abkn->arnm", turned, inverse_first[:, :, :, :lower], precision=precise
        )
        return (signal / (first * second)).reshape(2, rows, lower * second)
    signal = jnp.einsum("brkm,bkn->rnm", turned, inverse_first[0][:, :, :lower], precision=precise)
    return (signal / (first * second)).reshape(rows, lower * second)


def complex_product(left, right):
    return jnp.stack(
        [left[0] * right[0] - left[1] * right[1], left[0] * right[1] + left[1] * right[0]]
    )


def conjugate_product(left, right):
    return jnp.stack(
        [left[0] * right[0] + left[1] * right[1], left[0] * right[1] - left[1] * right[0]]
    )


def mirror(array, seq_dim):
    moved = array
    for bit_index in range(lax.axis_size("seq").bit_length() - 1):
        moved = swapped(moved, "seq", bit_index)
    return jnp.flip(moved, axis=seq_dim)


def to_channels(stacked):
    return lax.all_to_all(stacked, "seq", split_axis=1, concat_axis=2, tiled=True)


def to_tokens(stacked):
    return lax.all_to_all(stacked, "seq", split_axis=2, concat_axis=1, tiled=True)


def body(tokens, w_query, w_value, w_out, long_filter, cotangent):
    floats = jnp.float32
    halves = jnp.bfloat16
    half = w_query.shape[0]
    seq_count = lax.axis_size("seq")
    batch_count = lax.axis_size("batch")
    length = tokens.shape[1] * seq_count
    first, second = split_sizes(length)
    tables = make_tables(first, second)
    scale = (2.0 * batch_count * length) ** (-0.5)
    source = tokens[0]
    front = source[:, :half]
    back = source[:, half:]
    back_strand = mirror(back, 0)[:, ::-1]
    strands = jnp.stack([front, back_strand])
    query = jnp.einsum("stk,kh->sht", strands, w_query, preferred_element_type=floats).astype(
        halves
    )
    value = jnp.einsum("stk,kh->sht", strands, w_value, preferred_element_type=floats).astype(
        halves
    )
    value_sig = to_channels(value).astype(floats)
    value_spec = forward_spectrum(value_sig, tables, first, second)
    taps_spec = forward_spectrum(
        jnp.stack([long_filter, jnp.zeros_like(long_filter)]), tables, first, second
    )
    conv_sig = inverse_spectrum(complex_product(value_spec, taps_spec), tables, first, second, True)
    conv_tok = to_tokens(conv_sig.astype(halves))
    gated = (query.astype(floats) * conv_tok.astype(floats)).astype(halves)
    gated_back = mirror(gated[1], 1)
    out_front = jnp.einsum("ht,hk->tk", gated[0], w_out, preferred_element_type=floats)
    out_back = jnp.einsum("ht,hk->tk", gated_back, w_out, preferred_element_type=floats)
    block_out = jnp.concatenate(
        [front.astype(floats) + out_front, back.astype(floats) + out_back[:, ::-1]], axis=1
    ).astype(halves)[None]
    upstream = cotangent[0]
    up_front = upstream[:, :half]
    up_back = upstream[:, half:]
    grad_back = mirror(up_back, 0)[:, ::-1]
    grad_strands = jnp.stack([up_front, grad_back])
    grad_gated = jnp.einsum(
        "stk,hk->sht", grad_strands, w_out, preferred_element_type=floats
    ).astype(halves)
    grad_query_t = (grad_gated.astype(floats) * conv_tok.astype(floats)).astype(halves)
    grad_conv = (grad_gated.astype(floats) * query.astype(floats)).astype(halves)
    grad_sig = to_channels(grad_conv).astype(floats)
    grad_spec = forward_spectrum(grad_sig, tables, first, second)
    value_grad_sig = inverse_spectrum(
        conjugate_product(taps_spec, grad_spec), tables, first, second, True
    )
    filter_part = (
        inverse_spectrum(conjugate_product(value_spec, grad_spec), tables, first, second, False)
        * scale
    )
    grad_value_t = to_tokens(value_grad_sig.astype(halves))
    front_in = jnp.einsum(
        "ht,kh->tk", grad_query_t[0], w_query, preferred_element_type=floats
    ) + jnp.einsum("ht,kh->tk", grad_value_t[0], w_value, preferred_element_type=floats)
    paired = jnp.stack([grad_query_t[1], grad_value_t[1]])
    paired = mirror(paired, 2)
    back_in = jnp.einsum(
        "ht,kh->tk", paired[0], w_query, preferred_element_type=floats
    ) + jnp.einsum("ht,kh->tk", paired[1], w_value, preferred_element_type=floats)
    grad_tokens = jnp.concatenate(
        [up_front.astype(floats) + front_in, up_back.astype(floats) + back_in[:, ::-1]], axis=1
    ).astype(halves)[None]
    term_query = jnp.einsum("stk,sht->kh", strands, grad_query_t, preferred_element_type=floats)
    term_value = jnp.einsum("stk,sht->kh", strands, grad_value_t, preferred_element_type=floats)
    term_out = jnp.einsum("sht,stk->hk", gated, grad_strands, preferred_element_type=floats)
    share = lax.psum_scatter(
        jnp.concatenate([term_query, term_value, term_out], axis=1) * scale,
        "seq",
        scatter_dimension=0,
        tiled=True,
    )
    share, filter_total = (
        lax.psum(share.astype(jnp.bfloat16), "batch").astype(jnp.float32),
        lax.psum(filter_part.astype(jnp.bfloat16), "batch").astype(jnp.float32),
    )
    return (
        block_out,
        grad_tokens,
        share[:, :half],
        share[:, half : 2 * half],
        share[:, 2 * half :],
        filter_total,
    )

MESH = pl.DeviceIdType.MESH


def angle_parts(length):
    step = 1 << (length.bit_length() - 1) // 2
    angle = np.pi * (np.arange(length) + 0.5)[None] / length
    coarse = np.arange(length // step)[:, None] * step * angle
    fine = np.arange(step)[:, None] * angle
    return (
        np.stack([np.cos(coarse), np.sin(coarse)]).astype(np.float32),
        np.stack([np.cos(fine), np.sin(fine)]).astype(np.float32),
    )


def matmul(left, right):
    return jnp.dot(left, right, preferred_element_type=jnp.float32)


def matmul_t(left, right):
    return lax.dot_general(
        left, right, (((1,), (1,)), ((), ())), preferred_element_type=jnp.float32
    )


def times(x, h, conj):
    size = x.shape[1] // 2
    xr, xs, hr, hs = x[:, :size], x[:, size:], h[:, :size], h[:, size:]
    if conj:
        return xr * hr + xs * hs, xs * hr - xr * hs
    return xr * hr - xs * hs, xr * hs + xs * hr


def fused(
    peers, scale,
    tok_in, wq_in, wv_in, wo_in, taps_in, cot_in, coarse_in, fine_in,
    block_out, grad_out, out_w, out_f,
    block, grad_tok, osem,
    tok, wq, wv, wo, taps, cot, coarse, fine, lsem,
    table, strands, ups, strands_t, query, gates, send1, recv1, send2, recv2,
    vspec, gspec, hspec, yspec,
    ssem1, rsem1, lsem1, ssem2, rsem2, lsem2,
    acc, kept, send_a, recv_a, send_b, recv_b, send_c, recv_c, full,
    acc_f, kept_f, send_af, recv_af, send_bf, recv_bf, full_f,
    ssem_a, rsem_a, ssem_b, rsem_b, ssem_c, rsem_c, ssem_d, rsem_d,
):
    me = lax.axis_index("seq")
    here, half = tok.shape[0], wq.shape[0]
    f32, b16 = jnp.float32, jnp.bfloat16
    own = half // peers
    length = here * peers

    barrier = pltpu.get_barrier_semaphore()
    for r in range(1, peers):
        pl.semaphore_signal(
            barrier, inc=1, device_id={"seq": lax.rem(me + r, peers)}, device_id_type=MESH
        )
    batches = lax.axis_size("batch")
    seat = lax.axis_index("batch")
    for r in range(1, batches):
        pl.semaphore_signal(
            barrier, inc=1, device_id={"batch": lax.rem(seat + r, batches)}, device_id_type=MESH
        )
    loads = {}
    pairs = (
        ("tok", tok_in, tok), ("wv", wv_in, wv), ("cot", cot_in, cot), ("wo", wo_in, wo),
        ("wq", wq_in, wq), ("coarse", coarse_in, coarse), ("fine", fine_in, fine),
        ("taps", taps_in, taps),
    )
    for index, (name, src, dst) in enumerate(pairs):
        loads[name] = pltpu.make_async_copy(src, dst, lsem.at[index])
        loads[name].start()
    low, high = lax.rem(seat, 2), seat // 2
    quarter = own // batches
    slot = 2 * low + high
    flip = (
        lax.broadcasted_iota(jnp.int32, (half, half), 0)
        + lax.broadcasted_iota(jnp.int32, (half, half), 1)
        == half - 1
    ).astype(f32).astype(b16)
    loads["tok"].wait()
    strands[:here] = tok[:, :half]
    strands[here:] = matmul(tok[:, half:], flip).astype(b16)
    loads["wv"].wait()
    value = matmul(strands[...], wv[...]).astype(b16)
    send1[0] = value[:here].T
    send1[1] = value[here:].T
    for name in ("cot", "wo", "wq"):
        loads[name].wait()
    ups[:here] = cot[:, :half]
    ups[here:] = matmul(cot[:, half:], flip).astype(b16)
    query[...] = matmul(strands[...], wq[...]).astype(b16)
    gates[...] = matmul_t(ups[...], wo[...]).astype(b16)
    grad_conv = (gates[...].astype(f32) * query[...].astype(f32)).astype(b16)
    send1[2] = grad_conv[:here].T
    send1[3] = grad_conv[here:].T
    pl.semaphore_wait(barrier, peers + batches - 2)

    def rows_of(p):
        return pl.ds(pl.multiple_of(p * own, own), own)

    def lanes_of(p):
        return pl.ds(pl.multiple_of(p * here, here), here)

    def out1(part):
        pair = pl.ds((0, 2, 3)[part], (2, 1, 1)[part])
        copies = []
        for r in range(1, peers):
            p = lax.rem(me + r, peers)
            copies.append(
                pltpu.make_async_remote_copy(
                    src_ref=send1.at[pair, rows_of(p), :],
                    dst_ref=recv1.at[pair, :, lanes_of(me)],
                    send_sem=ssem1.at[part, r],
                    recv_sem=rsem1.at[part, r],
                    device_id={"seq": p},
                    device_id_type=MESH,
                )
            )
        copies.append(
            pltpu.make_async_copy(
                send1.at[pair, rows_of(me), :], recv1.at[pair, :, lanes_of(me)], lsem1.at[part]
            )
        )
        for c in copies:
            c.start()
        return copies

    def out2(part):
        pair = pl.ds((0, 2, 3)[part], (2, 1, 1)[part])
        copies = []
        for r in range(1, peers):
            p = lax.rem(me + r, peers)
            copies.append(
                pltpu.make_async_remote_copy(
                    src_ref=send2.at[pair, :, lanes_of(p)],
                    dst_ref=recv2.at[pair, rows_of(me), :],
                    send_sem=ssem2.at[part, r],
                    recv_sem=rsem2.at[part, r],
                    device_id={"seq": p},
                    device_id_type=MESH,
                )
            )
        copies.append(
            pltpu.make_async_copy(
                send2.at[pair, :, lanes_of(me)], recv2.at[pair, rows_of(me), :], lsem2.at[part]
            )
        )
        for c in copies:
            c.start()
        return copies

    def part_of(bit, size):
        return pl.ds(pl.multiple_of(bit * size, size), size)

    def bundle(m):
        if m == 3:
            return acc_f, kept_f, send_af, recv_af, send_bf, recv_bf, full_f
        return (
            acc.at[m], kept.at[m], send_a.at[m], recv_a.at[m], send_b.at[m], recv_b.at[m], full.at[m]
        )

    def swap(src, dst, ssem, rsem, target):
        copy = pltpu.make_async_remote_copy(
            src_ref=src,
            dst_ref=dst,
            send_sem=ssem,
            recv_sem=rsem,
            device_id={"batch": target},
            device_id_type=MESH,
        )
        copy.start()
        return copy

    def stage_a(m):
        total, _, out, into, _, _, _ = bundle(m)
        out[...] = total[:, part_of(1 - low, 2 * quarter), :].astype(b16)
        return swap(out, into, ssem_a.at[m], rsem_a.at[m], 2 * high + 1 - low)

    def stage_b(m, copy):
        total, keep, _, arrived, out, into, _ = bundle(m)
        copy.wait()
        keep[...] = total[:, part_of(low, 2 * quarter), :] + arrived[...].astype(f32)
        out[...] = keep[:, part_of(1 - high, quarter), :].astype(b16)
        return swap(out, into, ssem_b.at[m], rsem_b.at[m], 2 * (1 - high) + low)

    def stage_c(m, copy):
        _, keep, _, _, _, arrived, _ = bundle(m)
        copy.wait()
        mine = (keep[:, part_of(high, quarter), :] + arrived[...].astype(f32)).astype(b16)
        if m == 3:
            full_f[slot] = mine[0]
            return None
        send_c[m] = mine
        copies = []
        for r in range(1, peers):
            p = lax.rem(me + r, peers)
            copies.append(
                pltpu.make_async_remote_copy(
                    src_ref=send_c.at[m, p],
                    dst_ref=recv_c.at[m, me],
                    send_sem=ssem_c.at[m, r],
                    recv_sem=rsem_c.at[m, r],
                    device_id={"seq": p},
                    device_id_type=MESH,
                )
            )
        for c in copies:
            c.start()
        recv_c[m, me] = send_c[m, me]
        return copies

    def stage_d(m, copies):
        whole = bundle(m)[-1]
        if m < 3:
            for c in copies:
                c.wait()
            whole[slot] = jnp.sum(recv_c[m].astype(f32), axis=0).astype(b16)
        return [
            swap(
                whole.at[slot], whole.at[slot], ssem_d.at[m, r], rsem_d.at[m, r],
                lax.rem(seat + r, batches),
            )
            for r in range(1, batches)
        ]

    def finish(m, copies):
        for c in copies:
            c.wait()
        target = out_f if m == 3 else out_w.at[m]
        return leave(m, bundle(m)[-1], target)

    def leave(index, src, dst):
        copy = pltpu.make_async_copy(src, dst, osem.at[index])
        copy.start()
        return copy

    def weight(m, left, right):
        acc[m] = (matmul(left, right) * scale).reshape(peers, own, half)

    first = out1(0)
    second = out1(1)
    for name in ("coarse", "fine", "taps"):
        loads[name].wait()

    count, step = coarse.shape[1], fine.shape[1]

    @pl.loop(0, count)
    def _(a):
        ca, sa = coarse[0, pl.ds(a, 1), :], coarse[1, pl.ds(a, 1), :]
        rows = pl.ds(pl.multiple_of(a * step, step), step)
        table[rows, :length] = (ca * fine[0] - sa * fine[1]).astype(b16)
        table[rows, length:] = (sa * fine[0] + ca * fine[1]).astype(b16)

    strands_t[...] = strands[...].T
    hspec[...] = matmul(taps[...].astype(b16), table[...])

    def product(row, spec, conj):
        r, s = times(spec[row, :], hspec[...], conj)
        yspec[row, :length] = r.astype(b16)
        yspec[row, length:] = s.astype(b16)

    def back_value(strand, copies):
        for c in copies:
            c.wait()
        row = pl.ds(strand * own, own)
        gspec[row, :] = matmul(recv1[2 + strand], table[...])
        product(row, gspec, strand == 0)
        send2[2 + strand] = (matmul_t(yspec[row, :], table[...]) * (1.0 / length)).astype(b16)
        return out2(1 + strand)

    for c in first:
        c.wait()
    vspec[...] = matmul(recv1[0:2].reshape(2 * own, length), table[...])
    product(pl.ds(0, own), vspec, False)
    product(pl.ds(own, own), vspec, True)
    conv_own = (matmul_t(yspec[...], table[...]) * (1.0 / length)).astype(b16)
    send2[0] = conv_own[:own]
    send2[1] = conv_own[own:]
    third = out2(0)
    late = out1(2)
    fourth = back_value(0, second)

    for c in third:
        c.wait()
    conv = jnp.concatenate([recv2[0].T, recv2[1].T], axis=0).astype(f32)
    grad_query = (gates[...].astype(f32) * conv).astype(b16)
    weight(0, strands_t[...], grad_query)
    a0 = stage_a(0)
    gated = (query[...].astype(f32) * conv).astype(b16)
    weight(1, gated.T, ups[...])
    a1 = stage_a(1)
    b0 = stage_b(0, a0)
    b1 = stage_b(1, a1)
    fifth = back_value(1, late)
    r0, s0 = times(gspec[:own, :], vspec[:own, :], True)
    r1, s1 = times(vspec[own:, :], gspec[own:, :], True)
    yspec[:own, :length] = (r0 + r1).astype(b16)
    yspec[:own, length:] = (s0 + s1).astype(b16)
    acc_f[0] = matmul_t(yspec[:own, :], table[...]) * (scale / length)
    af = stage_a(3)
    total = strands[...].astype(f32) + matmul(gated, wo[...])
    block[:, :half] = total[:here].astype(b16)
    block[:, half:] = matmul(total[here:].astype(b16), flip).astype(b16)
    o4 = leave(4, block, block_out)
    c0 = stage_c(0, b0)
    bf = stage_b(3, af)
    for c in fourth:
        c.wait()
    value_0 = recv2[2].T
    early = matmul(strands_t[:, :here], value_0)
    c1 = stage_c(1, b1)
    for c in fifth:
        c.wait()
    value_1 = recv2[3].T
    acc[2] = ((early + matmul(strands_t[:, here:], value_1)) * scale).reshape(peers, own, half)
    a2 = stage_a(2)
    stage_c(3, bf)
    b2 = stage_b(2, a2)
    grad_value = jnp.concatenate([value_0, value_1], axis=0)
    total = ups[...].astype(f32) + matmul_t(grad_query, wq[...]) + matmul_t(grad_value, wv[...])
    grad_tok[:, :half] = total[:here].astype(b16)
    grad_tok[:, half:] = matmul(total[here:].astype(b16), flip).astype(b16)
    o5 = leave(5, grad_tok, grad_out)
    c2 = stage_c(2, b2)
    df = stage_d(3, None)
    d0 = stage_d(0, c0)
    d1 = stage_d(1, c1)
    o3 = finish(3, df)
    o0 = finish(0, d0)
    o1 = finish(1, d1)
    d2 = stage_d(2, c2)
    o2 = finish(2, d2)
    for c in (o0, o1, o2, o3, o4, o5):
        c.wait()


def emit(block, grad_tok, weights, filters, block_out, grad_out, out_q, out_v, out_o, out_f):
    block_out[...] = block[...]
    grad_out[...] = grad_tok[...]
    out_q[...] = weights[0].reshape(out_q.shape).astype(out_q.dtype)
    out_o[...] = weights[1].reshape(out_o.shape).astype(out_o.dtype)
    out_v[...] = weights[2].reshape(out_v.shape).astype(out_v.dtype)
    out_f[...] = filters[...].reshape(out_f.shape).astype(out_f.dtype)


def short_body(tokens, w_query, w_value, w_out, long_filter, cotangent):
    f32, b16 = jnp.float32, jnp.bfloat16
    half = w_query.shape[0]
    peers = lax.axis_size("seq")
    here = tokens.shape[1]
    length = here * peers
    own = half // peers
    scale = (2.0 * lax.axis_size("batch") * length) ** (-0.5)
    coarse, fine = angle_parts(length)
    dma = pltpu.SemaphoreType.DMA
    batches = lax.axis_size("batch")
    quarter = own // batches
    vmem = pltpu.VMEM
    arguments = (tokens[0], w_query, w_value, w_out, long_filter, cotangent[0], coarse, fine)
    block, grad_tok, weights, filters = pl.pallas_call(
        functools.partial(fused, peers, scale),
        out_shape=(
            jax.ShapeDtypeStruct((here, 2 * half), b16),
            jax.ShapeDtypeStruct((here, 2 * half), b16),
            jax.ShapeDtypeStruct((3, batches, quarter, half), b16),
            jax.ShapeDtypeStruct((batches, quarter, length), b16),
        ),
        in_specs=[pl.BlockSpec(memory_space=pltpu.HBM)] * 8,
        out_specs=(pl.BlockSpec(memory_space=pltpu.HBM),) * 4,
        scratch_shapes=[
            vmem((here, 2 * half), b16),
            vmem((here, 2 * half), b16),
            dma((6,)),
            *(vmem(a.shape, a.dtype) for a in arguments),
            dma((8,)),
            pltpu.VMEM((length, 2 * length), b16),
            pltpu.VMEM((2 * here, half), b16),
            pltpu.VMEM((2 * here, half), b16),
            pltpu.VMEM((half, 2 * here), b16),
            pltpu.VMEM((2 * here, half), b16),
            pltpu.VMEM((2 * here, half), b16),
            pltpu.VMEM((4, half, here), b16),
            pltpu.VMEM((4, own, length), b16),
            pltpu.VMEM((4, own, length), b16),
            pltpu.VMEM((4, half, here), b16),
            pltpu.VMEM((2 * own, 2 * length), f32),
            pltpu.VMEM((2 * own, 2 * length), f32),
            pltpu.VMEM((own, 2 * length), f32),
            pltpu.VMEM((2 * own, 2 * length), b16),
            dma((3, peers)),
            dma((3, peers)),
            dma((3,)),
            dma((3, peers)),
            dma((3, peers)),
            dma((3,)),
            vmem((3, peers, own, half), f32),
            vmem((3, peers, 2 * quarter, half), f32),
            vmem((3, peers, 2 * quarter, half), b16),
            vmem((3, peers, 2 * quarter, half), b16),
            vmem((3, peers, quarter, half), b16),
            vmem((3, peers, quarter, half), b16),
            vmem((3, peers, quarter, half), b16),
            vmem((3, peers, quarter, half), b16),
            vmem((3, batches, quarter, half), b16),
            vmem((1, own, length), f32),
            vmem((1, 2 * quarter, length), f32),
            vmem((1, 2 * quarter, length), b16),
            vmem((1, 2 * quarter, length), b16),
            vmem((1, quarter, length), b16),
            vmem((1, quarter, length), b16),
            vmem((batches, quarter, length), b16),
            dma((4,)),
            dma((4,)),
            dma((4,)),
            dma((4,)),
            dma((3, peers)),
            dma((3, peers)),
            dma((4, batches)),
            dma((4, batches)),
        ],
        compiler_params=pltpu.CompilerParams(
            collective_id=0, has_side_effects=True, vmem_limit_bytes=65900000
        ),
    )(*arguments)
    block, grad_tok, *sums = pl.pallas_call(
        emit,
        out_shape=(
            jax.ShapeDtypeStruct((here, 2 * half), b16),
            jax.ShapeDtypeStruct((here, 2 * half), b16),
            jax.ShapeDtypeStruct((own, half), f32),
            jax.ShapeDtypeStruct((own, half), f32),
            jax.ShapeDtypeStruct((own, half), f32),
            jax.ShapeDtypeStruct((own, length), f32),
        ),
        in_specs=[pl.BlockSpec(memory_space=pltpu.VMEM)] * 4,
        out_specs=(pl.BlockSpec(memory_space=pltpu.VMEM),) * 6,
        compiler_params=pltpu.CompilerParams(vmem_limit_bytes=65900000),
    )(block, grad_tok, weights, filters)
    return (block[None], grad_tok[None], *sums)


def fits(tokens, half):
    peers, batches = lax.axis_size("seq"), lax.axis_size("batch")
    small = (tokens.shape[1] * peers) ** 2 * 4 <= 8 << 20
    return small and batches == 4 and half % (16 * batches * peers) == 0


def choose(tokens, *rest):
    short = fits(tokens, rest[0].shape[0])
    return (short_body if short else body)(tokens, *rest)


def solution(mesh):
    in_specs = (P("batch", "seq", None), P(), P(), P(), P("seq", None), P("batch", "seq", None))
    out_specs = (
        P("batch", "seq", None),
        P("batch", "seq", None),
        P("seq", None),
        P("seq", None),
        P("seq", None),
        P("seq", None),
    )
    return jax.shard_map(choose, mesh=mesh, in_specs=in_specs, out_specs=out_specs, check_vma=False)
```

profile of v0, /device:TPU:0, one launch (start us, length us, event | category | flops | bytes accessed | tf_op | source)
XLA Modules:
  0.0 55.8 jit_solution(2691083928115389029)
XLA Ops:
  0.6 53.0 %shard_map.127 = (bf16[128,1024]{1,0:T(8,128)(2,1)}, bf16[128,1024]{1,0:T(8,128)(2,1)}, bf16[3,4,16,512]{3,2,1,0:T(8,128)(2,1)}, bf16[4,16,1024]{2,1,0:T(8,128)(2,1)}) custom-call(bf16[128,1024]{1,0:T(8,128)(2,1)} %bitcast.4, bf16[512,512]{1,0:T(8,128)(2,1)} %wq_in.1, bf16[512,512]{1,0:T(8,128)(2,1)} %wv_in.1, bf16[512,512]{1,0:T(8,128)(2,1)} %wo_in.1, ...), custom_call_target="tpu_custom_call" | custom-call | tf_op jit(solution)/shard_map/pallas_call | solution.py:555
  53.6 2.1 %shard_map.128 = (bf16[128,1024]{1,0:T(8,128)(2,1)}, bf16[128,1024]{1,0:T(8,128)(2,1)}, f32[64,512]{1,0:T(8,128)}, f32[64,512]{1,0:T(8,128)}, f32[64,512]{1,0:T(8,128)}, /*index=5*/f32[64,1024]{1,0:T(8,128)}) custom-call(bf16[128,1024]{1,0:T(8,128)(2,1)} %get-tuple-element.16.block, bf16[128,1024]{1,0:T(8,128)(2,1)} %get-tuple-element.17.grad_tok, ...), custom_call_target="tpu_custom_call" | custom-call | tf_op jit(solution)/shard_map/pallas_call | solution.py:620
where the time goes:
time: 55.9 us; the launch traced here: 55.8 us
  Pallas kernels  55.1 us (99%)
  between operations  0.64 us (1%)
    pallas_call x1, Pallas kernels, short_body(): pl.pallas_call(functools.partial(fused, peers, scale), out_shape=(jax.Sha...  53 us
    pallas_call x1, Pallas kernels, short_body(): pl.pallas_call(emit, out_shape=(jax.ShapeDtypeStruct((here, 2 * half), b1...  2.15 us

commit v1 on v0

--- a/solution.py
+++ b/solution.py
@@ -226,59 +226,148 @@
 
 
 def fused(
-    peers, scale,
+    scale,
     tok_in, wq_in, wv_in, wo_in, taps_in, cot_in, coarse_in, fine_in,
     block_out, grad_out, out_w, out_f,
     block, grad_tok, osem,
     tok, wq, wv, wo, taps, cot, coarse, fine, lsem,
     table, strands, ups, strands_t, query, gates, send1, recv1, send2, recv2,
-    vspec, gspec, hspec, yspec,
-    ssem1, rsem1, lsem1, ssem2, rsem2, lsem2,
+    both_taps, vspec, gspec, hspec, yspec, fspec,
+    ssem1, rsem1, lsem1, ssem2, rsem2, lsem2, ssem_t, rsem_t,
     acc, kept, send_a, recv_a, send_b, recv_b, send_c, recv_c, full,
-    acc_f, kept_f, send_af, recv_af, send_bf, recv_bf, full_f,
+    acc_f, kept_f, last_f, send_af, recv_af, send_bf, recv_bf, send_cf, recv_cf, full_f,
     ssem_a, rsem_a, ssem_b, rsem_b, ssem_c, rsem_c, ssem_d, rsem_d,
 ):
-    me = lax.axis_index("seq")
+    peers, batches = lax.axis_size("seq"), lax.axis_size("batch")
+    me, seat = lax.axis_index("seq"), lax.axis_index("batch")
     here, half = tok.shape[0], wq.shape[0]
     f32, b16 = jnp.float32, jnp.bfloat16
     own = half // peers
     length = here * peers
+    quarter = own // batches
+    mates = peers // 2
+    wide = mates * here
+    rows = 2 * own
+    side, seat_in_side = me // mates, lax.rem(me, mates)
+    other = 1 - side
+    sign = (2 * side - 1).astype(f32)
+    column, level = lax.rem(me, 2), me // 2
+    levels = peers // 2
+    low, high = lax.rem(seat, 2), seat // 2
+    slot = 2 * low + high
 
     barrier = pltpu.get_barrier_semaphore()
+    across = me + 1 - 2 * column
+    facing = seat + 2 - 4 * high
     for r in range(1, peers):
         pl.semaphore_signal(
             barrier, inc=1, device_id={"seq": lax.rem(me + r, peers)}, device_id_type=MESH
         )
-    batches = lax.axis_size("batch")
-    seat = lax.axis_index("batch")
     for r in range(1, batches):
         pl.semaphore_signal(
             barrier, inc=1, device_id={"batch": lax.rem(seat + r, batches)}, device_id_type=MESH
         )
+    pl.semaphore_signal(
+        barrier, inc=1, device_id={"seq": across, "batch": facing}, device_id_type=MESH
+    )
     loads = {}
     pairs = (
-        ("tok", tok_in, tok), ("wv", wv_in, wv), ("cot", cot_in, cot), ("wo", wo_in, wo),
-        ("wq", wq_in, wq), ("coarse", coarse_in, coarse), ("fine", fine_in, fine),
-        ("taps", taps_in, taps),
+        ("tok", tok_in, tok), ("wv", wv_in, wv), ("taps", taps_in, taps), ("cot", cot_in, cot),
+        ("wo", wo_in, wo), ("wq", wq_in, wq), ("coarse", coarse_in, coarse), ("fine", fine_in, fine),
     )
     for index, (name, src, dst) in enumerate(pairs):
         loads[name] = pltpu.make_async_copy(src, dst, lsem.at[index])
         loads[name].start()
-    low, high = lax.rem(seat, 2), seat // 2
-    quarter = own // batches
-    slot = 2 * low + high
+
+    def remote(src, dst, ssem, rsem, **device):
+        copy = pltpu.make_async_remote_copy(
+            src_ref=src, dst_ref=dst, send_sem=ssem, recv_sem=rsem,
+            device_id=device, device_id_type=MESH,
+        )
+        copy.start()
+        return copy
+
+    def local(src, dst, sem):
+        copy = pltpu.make_async_copy(src, dst, sem)
+        copy.start()
+        return copy
+
+    def wait(copies):
+        for c in copies:
+            c.wait()
+
     flip = (
         lax.broadcasted_iota(jnp.int32, (half, half), 0)
         + lax.broadcasted_iota(jnp.int32, (half, half), 1)
         == half - 1
     ).astype(f32).astype(b16)
+
+    def stage_rows(index, x):
+        turned = x.T
+        for bh in range(2):
+            for bj in range(mates):
+                start = (bh * mates + bj) * own
+                send1[index, bj, bh] = turned[start : start + own]
+
     loads["tok"].wait()
     strands[:here] = tok[:, :half]
     strands[here:] = matmul(tok[:, half:], flip).astype(b16)
     loads["wv"].wait()
     value = matmul(strands[...], wv[...]).astype(b16)
-    send1[0] = value[:here].T
-    send1[1] = value[here:].T
+    stage_rows(0, value[:here])
+    stage_rows(1, value[here:])
+    loads["taps"].wait()
+    both_taps[pl.ds(side, 1)] = taps[...].astype(b16).reshape(1, batches, quarter, length)
+    pl.semaphore_wait(barrier, peers + batches - 1)
+
+    partner = lax.rem(me + mates, peers)
+    tap_copy = remote(
+        both_taps.at[side, seat], both_taps.at[side, seat], ssem_t.at[0], rsem_t.at[0], seq=partner
+    )
+
+    def out1_cross(d):
+        c = 2 * d + (side if d == 0 else other)
+        copies = []
+        for r in range(mates):
+            q = lax.rem(seat_in_side + r, mates)
+            copies.append(
+                remote(
+                    send1.at[c, q], recv1.at[c, me], ssem1.at[d, mates + r], rsem1.at[d, mates + r],
+                    seq=other * mates + q,
+                )
+            )
+        return copies
+
+    def out1_own(d):
+        pair = pl.ds(2 * d, 2)
+        copies = []
+        for r in range(1, mates):
+            q = lax.rem(seat_in_side + r, mates)
+            copies.append(
+                remote(
+                    send1.at[pair, q], recv1.at[pair, me], ssem1.at[d, r], rsem1.at[d, r],
+                    seq=side * mates + q,
+                )
+            )
+        copies.append(local(send1.at[pair, seat_in_side], recv1.at[pair, me], lsem1.at[d]))
+        return copies
+
+    def out2(k, c):
+        copies = []
+        for r in range(1, mates):
+            q = lax.rem(seat_in_side + r, mates)
+            copies.append(
+                remote(
+                    send2.at[c, q], recv2.at[c, seat_in_side], ssem2.at[k, r], rsem2.at[k, r],
+                    seq=side * mates + q,
+                )
+            )
+        copies.append(local(send2.at[c, seat_in_side], recv2.at[c, seat_in_side], lsem2.at[k]))
+        return copies
+
+    own_v = out1_own(0)
+    cross_v = out1_cross(0)
+
     for name in ("cot", "wo", "wq"):
         loads[name].wait()
     ups[:here] = cot[:, :half]
@@ -286,247 +375,208 @@
     query[...] = matmul(strands[...], wq[...]).astype(b16)
     gates[...] = matmul_t(ups[...], wo[...]).astype(b16)
     grad_conv = (gates[...].astype(f32) * query[...].astype(f32)).astype(b16)
-    send1[2] = grad_conv[:here].T
-    send1[3] = grad_conv[here:].T
-    pl.semaphore_wait(barrier, peers + batches - 2)
-
-    def rows_of(p):
-        return pl.ds(pl.multiple_of(p * own, own), own)
-
-    def lanes_of(p):
-        return pl.ds(pl.multiple_of(p * here, here), here)
-
-    def out1(part):
-        pair = pl.ds((0, 2, 3)[part], (2, 1, 1)[part])
+    stage_rows(2, grad_conv[:here])
+    stage_rows(3, grad_conv[here:])
+    own_g = out1_own(1)
+    cross_g = out1_cross(1)
+
+    for name in ("coarse", "fine"):
+        loads[name].wait()
+    count, step = coarse.shape[1], fine.shape[1]
+
+    @pl.loop(0, count)
+    def _(a):
+        ca, sa = coarse[0, pl.ds(a, 1), :], coarse[1, pl.ds(a, 1), :]
+        at = pl.ds(pl.multiple_of(a * step, step), step)
+        table[at, :length] = (ca * fine[0] - sa * fine[1]).astype(b16)
+        table[at, length:] = (sa * fine[0] + ca * fine[1]).astype(b16)
+
+    tap_copy.wait()
+    tap_copies = [
+        remote(
+            both_taps.at[other, seat], both_taps.at[other, seat], ssem_t.at[r], rsem_t.at[r],
+            batch=lax.rem(seat + r, batches),
+        )
+        for r in range(1, batches)
+    ]
+    strands_t[...] = strands[...].T
+
+    def rows_at(i):
+        return pl.ds(pl.multiple_of(i * rows, rows), rows)
+
+    def table_of(which):
+        return table[pl.ds(pl.multiple_of(which * wide, wide), wide), :]
+
+    def signal(c, which):
+        return jnp.concatenate(
+            [recv1[c, which * mates + i].reshape(rows, here) for i in range(mates)], axis=1
+        )
+
+    def own_signals(d):
+        return jnp.concatenate([signal(2 * d, side), signal(2 * d + 1, side)], axis=0)
+
+    def returned(k, c, spec, conj):
+        r, s = times(spec, hspec[...], conj)
+        yspec[k, :, :length] = r.astype(b16)
+        yspec[k, :, length:] = s.astype(b16)
+        back = (matmul_t(yspec[k], table_of(side)) * (1.0 / length)).astype(b16)
+        for q in range(mates):
+            send2[pl.ds(c, 1), q] = back[:, q * here : (q + 1) * here].reshape(1, 2, own, here)
+        return out2(k, c)
+
+    wait(own_v)
+    vspec[...] = matmul(own_signals(0), table_of(side))
+    wait(tap_copies)
+    hspec[...] = matmul(both_taps[...].reshape(rows, length), table[...])
+    hspec[:, length:] = hspec[:, length:] * sign
+    self_v = returned(0, side, vspec[rows_at(side), :], True)
+    wait(cross_v)
+    vspec[rows_at(other), :] = vspec[rows_at(other), :] + matmul(
+        signal(other, other), table_of(other)
+    )
+    full_v = returned(1, other, vspec[rows_at(other), :], False)
+
+    wait(own_g)
+    gspec[...] = matmul(own_signals(1), table_of(side))
+    self_g = returned(2, 2 + other, gspec[rows_at(other), :], True)
+    r0, s0 = times(gspec[rows_at(other), :], vspec[rows_at(other), :], True)
+    r1, s1 = times(gspec[rows_at(side), :], vspec[rows_at(side), :], True)
+    fspec[:, :length] = (r0 + r1).astype(b16)
+    fspec[:, length:] = ((s0 - s1) * sign).astype(b16)
+    wait(cross_g)
+    gspec[rows_at(side), :] = gspec[rows_at(side), :] + matmul(
+        signal(2 + side, other), table_of(other)
+    )
+    full_g = returned(3, 2 + side, gspec[rows_at(side), :], False)
+
+    def part_of(bit, size):
+        return pl.ds(pl.multiple_of(bit * size, size), size)
+
+    def weight(m, product):
+        acc[m] = (product * scale).reshape(levels, 2, own, half)
+
+    def stage_a(m):
+        send_a[m] = acc[m, :, :, part_of(1 - low, 2 * quarter), :].astype(b16)
+        return remote(
+            send_a.at[m], recv_a.at[m], ssem_a.at[m], rsem_a.at[m], batch=2 * high + 1 - low
+        )
+
+    def stage_b(m, copy):
+        copy.wait()
+
+        def pick(x, y):
+            at = pl.ds(pl.multiple_of((2 * low + y) * quarter, quarter), quarter)
+            mine = acc[m, :, pl.ds(x, 1), at, :]
+            theirs = recv_a[m, :, pl.ds(x, 1), part_of(y, quarter), :].astype(f32)
+            return (mine + theirs).reshape(levels, quarter, half)
+
         copies = []
-        for r in range(1, peers):
-            p = lax.rem(me + r, peers)
+        for index, (dx, dy) in enumerate(((1, 1), (1, 0), (0, 1))):
+            x = 1 - column if dx else column
+            y = 1 - high if dy else high
+            send_b[m, index] = pick(x, y).astype(b16)
             copies.append(
-                pltpu.make_async_remote_copy(
-                    src_ref=send1.at[pair, rows_of(p), :],
-                    dst_ref=recv1.at[pair, :, lanes_of(me)],
-                    send_sem=ssem1.at[part, r],
-                    recv_sem=rsem1.at[part, r],
-                    device_id={"seq": p},
-                    device_id_type=MESH,
+                remote(
+                    send_b.at[m, index], recv_b.at[m, index], ssem_b.at[m, index],
+                    rsem_b.at[m, index], seq=across if dx else me, batch=facing if dy else seat,
                 )
             )
-        copies.append(
-            pltpu.make_async_copy(
-                send1.at[pair, rows_of(me), :], recv1.at[pair, :, lanes_of(me)], lsem1.at[part]
-            )
-        )
-        for c in copies:
-            c.start()
+        kept[m] = pick(column, high)
         return copies
 
-    def out2(part):
-        pair = pl.ds((0, 2, 3)[part], (2, 1, 1)[part])
+    def stage_c(m, copies):
+        wait(copies)
+        send_c[m] = (kept[m] + jnp.sum(recv_b[m].astype(f32), axis=0)).astype(b16)
         copies = []
-        for r in range(1, peers):
-            p = lax.rem(me + r, peers)
+        for r in range(1, levels):
+            z = lax.rem(level + r, levels)
             copies.append(
-                pltpu.make_async_remote_copy(
-                    src_ref=send2.at[pair, :, lanes_of(p)],
-                    dst_ref=recv2.at[pair, rows_of(me), :],
-                    send_sem=ssem2.at[part, r],
-                    recv_sem=rsem2.at[part, r],
-                    device_id={"seq": p},
-                    device_id_type=MESH,
+                remote(
+                    send_c.at[m, z], recv_c.at[m, level], ssem_c.at[m, r], rsem_c.at[m, r],
+                    seq=2 * z + column,
                 )
             )
-        copies.append(
-            pltpu.make_async_copy(
-                send2.at[pair, :, lanes_of(me)], recv2.at[pair, rows_of(me), :], lsem2.at[part]
-            )
-        )
-        for c in copies:
-            c.start()
+        recv_c[m, level] = send_c[m, level]
         return copies
 
-    def part_of(bit, size):
-        return pl.ds(pl.multiple_of(bit * size, size), size)
-
-    def bundle(m):
-        if m == 3:
-            return acc_f, kept_f, send_af, recv_af, send_bf, recv_bf, full_f
-        return (
-            acc.at[m], kept.at[m], send_a.at[m], recv_a.at[m], send_b.at[m], recv_b.at[m], full.at[m]
-        )
-
-    def swap(src, dst, ssem, rsem, target):
-        copy = pltpu.make_async_remote_copy(
-            src_ref=src,
-            dst_ref=dst,
-            send_sem=ssem,
-            recv_sem=rsem,
-            device_id={"batch": target},
-            device_id_type=MESH,
-        )
-        copy.start()
-        return copy
-
-    def stage_a(m):
-        total, _, out, into, _, _, _ = bundle(m)
-        out[...] = total[:, part_of(1 - low, 2 * quarter), :].astype(b16)
-        return swap(out, into, ssem_a.at[m], rsem_a.at[m], 2 * high + 1 - low)
-
-    def stage_b(m, copy):
-        total, keep, _, arrived, out, into, _ = bundle(m)
-        copy.wait()
-        keep[...] = total[:, part_of(low, 2 * quarter), :] + arrived[...].astype(f32)
-        out[...] = keep[:, part_of(1 - high, quarter), :].astype(b16)
-        return swap(out, into, ssem_b.at[m], rsem_b.at[m], 2 * (1 - high) + low)
-
-    def stage_c(m, copy):
-        _, keep, _, _, _, arrived, _ = bundle(m)
-        copy.wait()
-        mine = (keep[:, part_of(high, quarter), :] + arrived[...].astype(f32)).astype(b16)
-        if m == 3:
-            full_f[slot] = mine[0]
-            return None
-        send_c[m] = mine
-        copies = []
-        for r in range(1, peers):
-            p = lax.rem(me + r, peers)
-            copies.append(
-                pltpu.make_async_remote_copy(
-                    src_ref=send_c.at[m, p],
-                    dst_ref=recv_c.at[m, me],
-                    send_sem=ssem_c.at[m, r],
-                    recv_sem=rsem_c.at[m, r],
-                    device_id={"seq": p},
-                    device_id_type=MESH,
-                )
-            )
-        for c in copies:
-            c.start()
-        recv_c[m, me] = send_c[m, me]
-        return copies
-
-    def stage_d(m, copies):
-        whole = bundle(m)[-1]
-        if m < 3:
-            for c in copies:
-                c.wait()
-            whole[slot] = jnp.sum(recv_c[m].astype(f32), axis=0).astype(b16)
+    def share(m, whole):
         return [
-            swap(
+            remote(
                 whole.at[slot], whole.at[slot], ssem_d.at[m, r], rsem_d.at[m, r],
-                lax.rem(seat + r, batches),
+                batch=lax.rem(seat + r, batches),
             )
             for r in range(1, batches)
         ]
 
+    def stage_d(m, copies):
+        wait(copies)
+        full[m, slot] = jnp.sum(recv_c[m].astype(f32), axis=0).astype(b16)
+        return share(m, full.at[m])
+
+    def leave(index, src, dst):
+        return local(src, dst, osem.at[index])
+
     def finish(m, copies):
-        for c in copies:
-            c.wait()
-        target = out_f if m == 3 else out_w.at[m]
-        return leave(m, bundle(m)[-1], target)
-
-    def leave(index, src, dst):
-        copy = pltpu.make_async_copy(src, dst, osem.at[index])
-        copy.start()
-        return copy
-
-    def weight(m, left, right):
-        acc[m] = (matmul(left, right) * scale).reshape(peers, own, half)
-
-    first = out1(0)
-    second = out1(1)
-    for name in ("coarse", "fine", "taps"):
-        loads[name].wait()
-
-    count, step = coarse.shape[1], fine.shape[1]
-
-    @pl.loop(0, count)
-    def _(a):
-        ca, sa = coarse[0, pl.ds(a, 1), :], coarse[1, pl.ds(a, 1), :]
-        rows = pl.ds(pl.multiple_of(a * step, step), step)
-        table[rows, :length] = (ca * fine[0] - sa * fine[1]).astype(b16)
-        table[rows, length:] = (sa * fine[0] + ca * fine[1]).astype(b16)
-
-    strands_t[...] = strands[...].T
-    hspec[...] = matmul(taps[...].astype(b16), table[...])
-
-    def product(row, spec, conj):
-        r, s = times(spec[row, :], hspec[...], conj)
-        yspec[row, :length] = r.astype(b16)
-        yspec[row, length:] = s.astype(b16)
-
-    def back_value(strand, copies):
-        for c in copies:
-            c.wait()
-        row = pl.ds(strand * own, own)
-        gspec[row, :] = matmul(recv1[2 + strand], table[...])
-        product(row, gspec, strand == 0)
-        send2[2 + strand] = (matmul_t(yspec[row, :], table[...]) * (1.0 / length)).astype(b16)
-        return out2(1 + strand)
-
-    for c in first:
-        c.wait()
-    vspec[...] = matmul(recv1[0:2].reshape(2 * own, length), table[...])
-    product(pl.ds(0, own), vspec, False)
-    product(pl.ds(own, own), vspec, True)
-    conv_own = (matmul_t(yspec[...], table[...]) * (1.0 / length)).astype(b16)
-    send2[0] = conv_own[:own]
-    send2[1] = conv_own[own:]
-    third = out2(0)
-    late = out1(2)
-    fourth = back_value(0, second)
-
-    for c in third:
-        c.wait()
-    conv = jnp.concatenate([recv2[0].T, recv2[1].T], axis=0).astype(f32)
+        wait(copies)
+        return leave(m, full_f if m == 3 else full.at[m], out_f if m == 3 else out_w.at[m])
+
+    wait(self_v)
+    wait(full_v)
+
+    def rejoin(c):
+        return jnp.concatenate(
+            [recv2[c, bj, bh] for bh in range(2) for bj in range(mates)], axis=0
+        ).T
+
+    conv = jnp.concatenate([rejoin(0), rejoin(1)], axis=0).astype(f32)
     grad_query = (gates[...].astype(f32) * conv).astype(b16)
-    weight(0, strands_t[...], grad_query)
+    weight(0, matmul(strands_t[...], grad_query))
     a0 = stage_a(0)
     gated = (query[...].astype(f32) * conv).astype(b16)
-    weight(1, gated.T, ups[...])
+    weight(1, matmul(gated.T, ups[...]))
     a1 = stage_a(1)
     b0 = stage_b(0, a0)
     b1 = stage_b(1, a1)
-    fifth = back_value(1, late)
-    r0, s0 = times(gspec[:own, :], vspec[:own, :], True)
-    r1, s1 = times(vspec[own:, :], gspec[own:, :], True)
-    yspec[:own, :length] = (r0 + r1).astype(b16)
-    yspec[:own, length:] = (s0 + s1).astype(b16)
-    acc_f[0] = matmul_t(yspec[:own, :], table[...]) * (scale / length)
-    af = stage_a(3)
+    acc_f[...] = (matmul_t(fspec[...], table[...]) * (scale / length)).reshape(2, own, length)
+    send_af[...] = acc_f[:, part_of(1 - low, 2 * quarter), :].astype(b16)
+    af = remote(send_af, recv_af, ssem_a.at[3], rsem_a.at[3], batch=2 * high + 1 - low)
+    wait(self_g)
+    wait(full_g)
+    value_0, value_1 = rejoin(2), rejoin(3)
+    grad_value = jnp.concatenate([value_0, value_1], axis=0)
+    weight(2, matmul(strands_t[...], grad_value))
+    a2 = stage_a(2)
+    c0 = stage_c(0, b0)
+    c1 = stage_c(1, b1)
+    af.wait()
+    kept_f[...] = acc_f[:, part_of(low, 2 * quarter), :] + recv_af[...].astype(f32)
+    send_bf[...] = kept_f[:, part_of(1 - high, quarter), :].astype(b16)
+    bf = remote(send_bf, recv_bf, ssem_b.at[3, 0], rsem_b.at[3, 0], batch=facing)
+    b2 = stage_b(2, a2)
     total = strands[...].astype(f32) + matmul(gated, wo[...])
     block[:, :half] = total[:here].astype(b16)
     block[:, half:] = matmul(total[here:].astype(b16), flip).astype(b16)
     o4 = leave(4, block, block_out)
-    c0 = stage_c(0, b0)
-    bf = stage_b(3, af)
-    for c in fourth:
-        c.wait()
-    value_0 = recv2[2].T
-    early = matmul(strands_t[:, :here], value_0)
-    c1 = stage_c(1, b1)
-    for c in fifth:
-        c.wait()
-    value_1 = recv2[3].T
-    acc[2] = ((early + matmul(strands_t[:, here:], value_1)) * scale).reshape(peers, own, half)
-    a2 = stage_a(2)
-    stage_c(3, bf)
-    b2 = stage_b(2, a2)
-    grad_value = jnp.concatenate([value_0, value_1], axis=0)
+    bf.wait()
+    last_f[...] = kept_f[:, part_of(high, quarter), :] + recv_bf[...].astype(f32)
+    send_cf[...] = last_f[other].astype(b16)
+    cf = remote(send_cf, recv_cf, ssem_c.at[3, 0], rsem_c.at[3, 0], seq=partner)
+    c2 = stage_c(2, b2)
+    d0 = stage_d(0, c0)
+    d1 = stage_d(1, c1)
     total = ups[...].astype(f32) + matmul_t(grad_query, wq[...]) + matmul_t(grad_value, wv[...])
     grad_tok[:, :half] = total[:here].astype(b16)
     grad_tok[:, half:] = matmul(total[here:].astype(b16), flip).astype(b16)
     o5 = leave(5, grad_tok, grad_out)
-    c2 = stage_c(2, b2)
-    df = stage_d(3, None)
-    d0 = stage_d(0, c0)
-    d1 = stage_d(1, c1)
-    o3 = finish(3, df)
+    cf.wait()
+    full_f[slot] = (last_f[side] + recv_cf[...].astype(f32)).astype(b16)
+    df = share(3, full_f)
+    d2 = stage_d(2, c2)
     o0 = finish(0, d0)
     o1 = finish(1, d1)
-    d2 = stage_d(2, c2)
+    o3 = finish(3, df)
     o2 = finish(2, d2)
-    for c in (o0, o1, o2, o3, o4, o5):
-        c.wait()
+    wait((o0, o1, o2, o3, o4, o5))
 
 
 def emit(block, grad_tok, weights, filters, block_out, grad_out, out_q, out_v, out_o, out_f):
@@ -550,10 +600,11 @@
     dma = pltpu.SemaphoreType.DMA
     batches = lax.axis_size("batch")
     quarter = own // batches
+    mates = levels = peers // 2
     vmem = pltpu.VMEM
     arguments = (tokens[0], w_query, w_value, w_out, long_filter, cotangent[0], coarse, fine)
     block, grad_tok, weights, filters = pl.pallas_call(
-        functools.partial(fused, peers, scale),
+        functools.partial(fused, scale),
         out_shape=(
             jax.ShapeDtypeStruct((here, 2 * half), b16),
             jax.ShapeDtypeStruct((here, 2 * half), b16),
@@ -568,48 +619,55 @@
             dma((6,)),
             *(vmem(a.shape, a.dtype) for a in arguments),
             dma((8,)),
-            pltpu.VMEM((length, 2 * length), b16),
-            pltpu.VMEM((2 * here, half), b16),
-            pltpu.VMEM((2 * here, half), b16),
-            pltpu.VMEM((half, 2 * here), b16),
-            pltpu.VMEM((2 * here, half), b16),
-            pltpu.VMEM((2 * here, half), b16),
-            pltpu.VMEM((4, half, here), b16),
-            pltpu.VMEM((4, own, length), b16),
-            pltpu.VMEM((4, own, length), b16),
-            pltpu.VMEM((4, half, here), b16),
-            pltpu.VMEM((2 * own, 2 * length), f32),
-            pltpu.VMEM((2 * own, 2 * length), f32),
-            pltpu.VMEM((own, 2 * length), f32),
-            pltpu.VMEM((2 * own, 2 * length), b16),
-            dma((3, peers)),
-            dma((3, peers)),
-            dma((3,)),
-            dma((3, peers)),
-            dma((3, peers)),
-            dma((3,)),
-            vmem((3, peers, own, half), f32),
-            vmem((3, peers, 2 * quarter, half), f32),
-            vmem((3, peers, 2 * quarter, half), b16),
-            vmem((3, peers, 2 * quarter, half), b16),
-            vmem((3, peers, quarter, half), b16),
-            vmem((3, peers, quarter, half), b16),
-            vmem((3, peers, quarter, half), b16),
-            vmem((3, peers, quarter, half), b16),
+            vmem((length, 2 * length), b16),
+            vmem((2 * here, half), b16),
+            vmem((2 * here, half), b16),
+            vmem((half, 2 * here), b16),
+            vmem((2 * here, half), b16),
+            vmem((2 * here, half), b16),
+            vmem((4, mates, 2, own, here), b16),
+            vmem((4, peers, 2, own, here), b16),
+            vmem((4, mates, 2, own, here), b16),
+            vmem((4, mates, 2, own, here), b16),
+            vmem((2, batches, quarter, length), b16),
+            vmem((4 * own, 2 * length), f32),
+            vmem((4 * own, 2 * length), f32),
+            vmem((2 * own, 2 * length), f32),
+            vmem((4, 2 * own, 2 * length), b16),
+            vmem((2 * own, 2 * length), b16),
+            dma((2, peers)),
+            dma((2, peers)),
+            dma((2,)),
+            dma((4, mates)),
+            dma((4, mates)),
+            dma((4,)),
+            dma((batches,)),
+            dma((batches,)),
+            vmem((3, levels, 2, own, half), f32),
+            vmem((3, levels, quarter, half), f32),
+            vmem((3, levels, 2, 2 * quarter, half), b16),
+            vmem((3, levels, 2, 2 * quarter, half), b16),
+            vmem((3, 3, levels, quarter, half), b16),
+            vmem((3, 3, levels, quarter, half), b16),
+            vmem((3, levels, quarter, half), b16),
+            vmem((3, levels, quarter, half), b16),
             vmem((3, batches, quarter, half), b16),
-            vmem((1, own, length), f32),
-            vmem((1, 2 * quarter, length), f32),
-            vmem((1, 2 * quarter, length), b16),
-            vmem((1, 2 * quarter, length), b16),
-            vmem((1, quarter, length), b16),
-            vmem((1, quarter, length), b16),
+            vmem((2, own, length), f32),
+            vmem((2, 2 * quarter, length), f32),
+            vmem((2, quarter, length), f32),
+            vmem((2, 2 * quarter, length), b16),
+            vmem((2, 2 * quarter, length), b16),
+            vmem((2, quarter, length), b16),
+            vmem((2, quarter, length), b16),
+            vmem((quarter, length), b16),
+            vmem((quarter, length), b16),
             vmem((batches, quarter, length), b16),
             dma((4,)),
             dma((4,)),
-            dma((4,)),
-            dma((4,)),
-            dma((3, peers)),
-            dma((3, peers)),
+            dma((4, 3)),
+            dma((4, 3)),
+            dma((4, levels)),
+            dma((4, levels)),
             dma((4, batches)),
             dma((4, batches)),
         ],
@@ -637,7 +695,8 @@
 def fits(tokens, half):
     peers, batches = lax.axis_size("seq"), lax.axis_size("batch")
     small = (tokens.shape[1] * peers) ** 2 * 4 <= 8 << 20
-    return small and batches == 4 and half % (16 * batches * peers) == 0
+    square = peers == 8 and batches == 4 and tokens.shape[1] % 128 == 0
+    return small and square and half % (16 * batches * peers) == 0
 
 
 def choose(tokens, *rest):

time: 55.9 us -> 50.8 us (0.909)
  Pallas kernels: 55.1 us -> 50 us
    pallas_call x1, Pallas kernels: 53 us -> 47.8 us  [short_body(): pl.pallas_call(functools.partial(fused, scale), out_shape=(jax.ShapeDtype...]
where the time goes in v1:
time: 50.8 us; the launch traced here: 50.6 us
  Pallas kernels  50 us (98%)
  between operations  0.64 us (1%)
    pallas_call x1, Pallas kernels, short_body(): pl.pallas_call(functools.partial(fused, scale), out_shape=(jax.ShapeDtype...  47.8 us
    pallas_call x1, Pallas kernels, short_body(): pl.pallas_call(emit, out_shape=(jax.ShapeDtypeStruct((here, 2 * half), b1...  2.15 us

profile of v1, /device:TPU:0, one launch (start us, length us, event | category | flops | bytes accessed | tf_op | source)
XLA Modules:
  0.0 50.6 jit_solution(6290692222151912540)
XLA Ops:
  0.6 47.8 %shard_map.127 = (bf16[128,1024]{1,0:T(8,128)(2,1)}, bf16[128,1024]{1,0:T(8,128)(2,1)}, bf16[3,4,16,512]{3,2,1,0:T(8,128)(2,1)}, bf16[4,16,1024]{2,1,0:T(8,128)(2,1)}) custom-call(bf16[128,1024]{1,0:T(8,128)(2,1)} %bitcast.4, bf16[512,512]{1,0:T(8,128)(2,1)} %wq_in.1, bf16[512,512]{1,0:T(8,128)(2,1)} %wv_in.1, bf16[512,512]{1,0:T(8,128)(2,1)} %wo_in.1, ...), custom_call_target="tpu_custom_call" | custom-call | tf_op jit(solution)/shard_map/pallas_call | solution.py:606
  48.5 2.1 %shard_map.128 = (bf16[128,1024]{1,0:T(8,128)(2,1)}, bf16[128,1024]{1,0:T(8,128)(2,1)}, f32[64,512]{1,0:T(8,128)}, f32[64,512]{1,0:T(8,128)}, f32[64,512]{1,0:T(8,128)}, /*index=5*/f32[64,1024]{1,0:T(8,128)}) custom-call(bf16[128,1024]{1,0:T(8,128)(2,1)} %get-tuple-element.16.block, bf16[128,1024]{1,0:T(8,128)(2,1)} %get-tuple-element.17.grad_tok, ...), custom_call_target="tpu_custom_call" | custom-call | tf_op jit(solution)/shard_map/pallas_call | solution.py:678

commit v2 on v1

--- a/solution.py
+++ b/solution.py
@@ -424,31 +424,6 @@
             send2[pl.ds(c, 1), q] = back[:, q * here : (q + 1) * here].reshape(1, 2, own, here)
         return out2(k, c)
 
-    wait(own_v)
-    vspec[...] = matmul(own_signals(0), table_of(side))
-    wait(tap_copies)
-    hspec[...] = matmul(both_taps[...].reshape(rows, length), table[...])
-    hspec[:, length:] = hspec[:, length:] * sign
-    self_v = returned(0, side, vspec[rows_at(side), :], True)
-    wait(cross_v)
-    vspec[rows_at(other), :] = vspec[rows_at(other), :] + matmul(
-        signal(other, other), table_of(other)
-    )
-    full_v = returned(1, other, vspec[rows_at(other), :], False)
-
-    wait(own_g)
-    gspec[...] = matmul(own_signals(1), table_of(side))
-    self_g = returned(2, 2 + other, gspec[rows_at(other), :], True)
-    r0, s0 = times(gspec[rows_at(other), :], vspec[rows_at(other), :], True)
-    r1, s1 = times(gspec[rows_at(side), :], vspec[rows_at(side), :], True)
-    fspec[:, :length] = (r0 + r1).astype(b16)
-    fspec[:, length:] = ((s0 - s1) * sign).astype(b16)
-    wait(cross_g)
-    gspec[rows_at(side), :] = gspec[rows_at(side), :] + matmul(
-        signal(2 + side, other), table_of(other)
-    )
-    full_g = returned(3, 2 + side, gspec[rows_at(side), :], False)
-
     def part_of(bit, size):
         return pl.ds(pl.multiple_of(bit * size, size), size)
 
@@ -520,14 +495,44 @@
         wait(copies)
         return leave(m, full_f if m == 3 else full.at[m], out_f if m == 3 else out_w.at[m])
 
-    wait(self_v)
-    wait(full_v)
-
     def rejoin(c):
         return jnp.concatenate(
             [recv2[c, bj, bh] for bh in range(2) for bj in range(mates)], axis=0
         ).T
 
+    wait(own_v)
+    vspec[...] = matmul(own_signals(0), table_of(side))
+    wait(tap_copies)
+    hspec[...] = matmul(both_taps[...].reshape(rows, length), table[...])
+    hspec[:, length:] = hspec[:, length:] * sign
+    self_v = returned(0, side, vspec[rows_at(side), :], True)
+    wait(cross_v)
+    vspec[rows_at(other), :] = vspec[rows_at(other), :] + matmul(
+        signal(other, other), table_of(other)
+    )
+    full_v = returned(1, other, vspec[rows_at(other), :], False)
+
+    wait(own_g)
+    gspec[...] = matmul(own_signals(1), table_of(side))
+    self_g = returned(2, 2 + other, gspec[rows_at(other), :], True)
+    r0, s0 = times(gspec[rows_at(other), :], vspec[rows_at(other), :], True)
+    r1, s1 = times(gspec[rows_at(side), :], vspec[rows_at(side), :], True)
+    fspec[:, :length] = (r0 + r1).astype(b16)
+    fspec[:, length:] = ((s0 - s1) * sign).astype(b16)
+    acc_f[...] = (matmul_t(fspec[...], table[...]) * (scale / length)).reshape(2, own, length)
+    send_af[...] = acc_f[:, part_of(1 - low, 2 * quarter), :].astype(b16)
+    af = remote(send_af, recv_af, ssem_a.at[3], rsem_a.at[3], batch=2 * high + 1 - low)
+    af.wait()
+    kept_f[...] = acc_f[:, part_of(low, 2 * quarter), :] + recv_af[...].astype(f32)
+    send_bf[...] = kept_f[:, part_of(1 - high, quarter), :].astype(b16)
+    bf = remote(send_bf, recv_bf, ssem_b.at[3, 0], rsem_b.at[3, 0], batch=facing)
+    wait(cross_g)
+    gspec[rows_at(side), :] = gspec[rows_at(side), :] + matmul(
+        signal(2 + side, other), table_of(other)
+    )
+    full_g = returned(3, 2 + side, gspec[rows_at(side), :], False)
+    wait(self_v)
+    wait(full_v)
     conv = jnp.concatenate([rejoin(0), rejoin(1)], axis=0).astype(f32)
     grad_query = (gates[...].astype(f32) * conv).astype(b16)
     weight(0, matmul(strands_t[...], grad_query))
@@ -536,45 +541,38 @@
     weight(1, matmul(gated.T, ups[...]))
     a1 = stage_a(1)
     b0 = stage_b(0, a0)
+    bf.wait()
+    last_f[...] = kept_f[:, part_of(high, quarter), :] + recv_bf[...].astype(f32)
+    send_cf[...] = last_f[other].astype(b16)
+    cf = remote(send_cf, recv_cf, ssem_c.at[3, 0], rsem_c.at[3, 0], seq=partner)
     b1 = stage_b(1, a1)
-    acc_f[...] = (matmul_t(fspec[...], table[...]) * (scale / length)).reshape(2, own, length)
-    send_af[...] = acc_f[:, part_of(1 - low, 2 * quarter), :].astype(b16)
-    af = remote(send_af, recv_af, ssem_a.at[3], rsem_a.at[3], batch=2 * high + 1 - low)
     wait(self_g)
     wait(full_g)
     value_0, value_1 = rejoin(2), rejoin(3)
     grad_value = jnp.concatenate([value_0, value_1], axis=0)
     weight(2, matmul(strands_t[...], grad_value))
     a2 = stage_a(2)
-    c0 = stage_c(0, b0)
-    c1 = stage_c(1, b1)
-    af.wait()
-    kept_f[...] = acc_f[:, part_of(low, 2 * quarter), :] + recv_af[...].astype(f32)
-    send_bf[...] = kept_f[:, part_of(1 - high, quarter), :].astype(b16)
-    bf = remote(send_bf, recv_bf, ssem_b.at[3, 0], rsem_b.at[3, 0], batch=facing)
-    b2 = stage_b(2, a2)
     total = strands[...].astype(f32) + matmul(gated, wo[...])
     block[:, :half] = total[:here].astype(b16)
+    b2 = stage_b(2, a2)
     block[:, half:] = matmul(total[here:].astype(b16), flip).astype(b16)
     o4 = leave(4, block, block_out)
-    bf.wait()
-    last_f[...] = kept_f[:, part_of(high, quarter), :] + recv_bf[...].astype(f32)
-    send_cf[...] = last_f[other].astype(b16)
-    cf = remote(send_cf, recv_cf, ssem_c.at[3, 0], rsem_c.at[3, 0], seq=partner)
-    c2 = stage_c(2, b2)
-    d0 = stage_d(0, c0)
-    d1 = stage_d(1, c1)
+    c0 = stage_c(0, b0)
+    cf.wait()
+    full_f[slot] = (last_f[side] + recv_cf[...].astype(f32)).astype(b16)
+    df = share(3, full_f)
+    c1 = stage_c(1, b1)
     total = ups[...].astype(f32) + matmul_t(grad_query, wq[...]) + matmul_t(grad_value, wv[...])
     grad_tok[:, :half] = total[:here].astype(b16)
     grad_tok[:, half:] = matmul(total[here:].astype(b16), flip).astype(b16)
     o5 = leave(5, grad_tok, grad_out)
-    cf.wait()
-    full_f[slot] = (last_f[side] + recv_cf[...].astype(f32)).astype(b16)
-    df = share(3, full_f)
+    d0 = stage_d(0, c0)
+    c2 = stage_c(2, b2)
+    d1 = stage_d(1, c1)
+    o3 = finish(3, df)
+    o0 = finish(0, d0)
     d2 = stage_d(2, c2)
-    o0 = finish(0, d0)
     o1 = finish(1, d1)
-    o3 = finish(3, df)
     o2 = finish(2, d2)
     wait((o0, o1, o2, o3, o4, o5))
 

time: 50.8 us -> 48.5 us (0.955)
  Pallas kernels: 50 us -> 47.7 us
    pallas_call x1, Pallas kernels: 47.8 us -> 45.6 us  [short_body(): pl.pallas_call(functools.partial(fused, scale), out_shape=(jax.ShapeDtype...]
where the time goes in v2:
time: 48.5 us; the launch traced here: 48.4 us
  Pallas kernels  47.7 us (98%)
  between operations  0.64 us (1%)
    pallas_call x1, Pallas kernels, short_body(): pl.pallas_call(functools.partial(fused, scale), out_shape=(jax.ShapeDtype...  45.6 us
    pallas_call x1, Pallas kernels, short_body(): pl.pallas_call(emit, out_shape=(jax.ShapeDtypeStruct((here, 2 * half), b1...  2.15 us

profile of v2, /device:TPU:0, one launch (start us, length us, event | category | flops | bytes accessed | tf_op | source)
XLA Modules:
  0.0 48.4 jit_solution(14271904462128706855)
XLA Ops:
  0.6 45.6 %shard_map.127 = (bf16[128,1024]{1,0:T(8,128)(2,1)}, bf16[128,1024]{1,0:T(8,128)(2,1)}, bf16[3,4,16,512]{3,2,1,0:T(8,128)(2,1)}, bf16[4,16,1024]{2,1,0:T(8,128)(2,1)}) custom-call(bf16[128,1024]{1,0:T(8,128)(2,1)} %bitcast.4, bf16[512,512]{1,0:T(8,128)(2,1)} %wq_in.1, bf16[512,512]{1,0:T(8,128)(2,1)} %wv_in.1, bf16[512,512]{1,0:T(8,128)(2,1)} %wo_in.1, ...), custom_call_target="tpu_custom_call" | custom-call | tf_op jit(solution)/shard_map/pallas_call | solution.py:604
  46.2 2.1 %shard_map.128 = (bf16[128,1024]{1,0:T(8,128)(2,1)}, bf16[128,1024]{1,0:T(8,128)(2,1)}, f32[64,512]{1,0:T(8,128)}, f32[64,512]{1,0:T(8,128)}, f32[64,512]{1,0:T(8,128)}, /*index=5*/f32[64,1024]{1,0:T(8,128)}) custom-call(bf16[128,1024]{1,0:T(8,128)(2,1)} %get-tuple-element.16.block, bf16[128,1024]{1,0:T(8,128)(2,1)} %get-tuple-element.17.grad_tok, ...), custom_call_target="tpu_custom_call" | custom-call | tf_op jit(solution)/shard_map/pallas_call | solution.py:676

commit v3 on v2

--- a/solution.py
+++ b/solution.py
@@ -229,13 +229,12 @@
     scale,
     tok_in, wq_in, wv_in, wo_in, taps_in, cot_in, coarse_in, fine_in,
     block_out, grad_out, out_w, out_f,
-    block, grad_tok, osem,
     tok, wq, wv, wo, taps, cot, coarse, fine, lsem,
     table, strands, ups, strands_t, query, gates, send1, recv1, send2, recv2,
     both_taps, vspec, gspec, hspec, yspec, fspec,
     ssem1, rsem1, lsem1, ssem2, rsem2, lsem2, ssem_t, rsem_t,
-    acc, kept, send_a, recv_a, send_b, recv_b, send_c, recv_c, full,
-    acc_f, kept_f, last_f, send_af, recv_af, send_bf, recv_bf, send_cf, recv_cf, full_f,
+    acc, kept, send_a, recv_a, send_b, recv_b, send_c, recv_c,
+    acc_f, kept_f, last_f, send_af, recv_af, send_bf, recv_bf, send_cf, recv_cf,
     ssem_a, rsem_a, ssem_b, rsem_b, ssem_c, rsem_c, ssem_d, rsem_d,
 ):
     peers, batches = lax.axis_size("seq"), lax.axis_size("batch")
@@ -485,15 +484,8 @@
 
     def stage_d(m, copies):
         wait(copies)
-        full[m, slot] = jnp.sum(recv_c[m].astype(f32), axis=0).astype(b16)
-        return share(m, full.at[m])
-
-    def leave(index, src, dst):
-        return local(src, dst, osem.at[index])
-
-    def finish(m, copies):
-        wait(copies)
-        return leave(m, full_f if m == 3 else full.at[m], out_f if m == 3 else out_w.at[m])
+        out_w[m, slot] = jnp.sum(recv_c[m].astype(f32), axis=0).astype(b16)
+        return share(m, out_w.at[m])
 
     def rejoin(c):
         return jnp.concatenate(
@@ -553,37 +545,48 @@
     weight(2, matmul(strands_t[...], grad_value))
     a2 = stage_a(2)
     total = strands[...].astype(f32) + matmul(gated, wo[...])
-    block[:, :half] = total[:here].astype(b16)
+    block_out[:, :half] = total[:here].astype(b16)
     b2 = stage_b(2, a2)
-    block[:, half:] = matmul(total[here:].astype(b16), flip).astype(b16)
-    o4 = leave(4, block, block_out)
+    block_out[:, half:] = matmul(total[here:].astype(b16), flip).astype(b16)
     c0 = stage_c(0, b0)
     cf.wait()
-    full_f[slot] = (last_f[side] + recv_cf[...].astype(f32)).astype(b16)
-    df = share(3, full_f)
+    out_f[slot] = (last_f[side] + recv_cf[...].astype(f32)).astype(b16)
+    df = share(3, out_f)
     c1 = stage_c(1, b1)
     total = ups[...].astype(f32) + matmul_t(grad_query, wq[...]) + matmul_t(grad_value, wv[...])
-    grad_tok[:, :half] = total[:here].astype(b16)
-    grad_tok[:, half:] = matmul(total[here:].astype(b16), flip).astype(b16)
-    o5 = leave(5, grad_tok, grad_out)
+    grad_out[:, :half] = total[:here].astype(b16)
+    grad_out[:, half:] = matmul(total[here:].astype(b16), flip).astype(b16)
     d0 = stage_d(0, c0)
     c2 = stage_c(2, b2)
     d1 = stage_d(1, c1)
-    o3 = finish(3, df)
-    o0 = finish(0, d0)
+    wait(df)
+    wait(d0)
     d2 = stage_d(2, c2)
-    o1 = finish(1, d1)
-    o2 = finish(2, d2)
-    wait((o0, o1, o2, o3, o4, o5))
-
-
-def emit(block, grad_tok, weights, filters, block_out, grad_out, out_q, out_v, out_o, out_f):
-    block_out[...] = block[...]
-    grad_out[...] = grad_tok[...]
-    out_q[...] = weights[0].reshape(out_q.shape).astype(out_q.dtype)
-    out_o[...] = weights[1].reshape(out_o.shape).astype(out_o.dtype)
-    out_v[...] = weights[2].reshape(out_v.shape).astype(out_v.dtype)
-    out_f[...] = filters[...].reshape(out_f.shape).astype(out_f.dtype)
+    wait(d1)
+    wait(d2)
+
+
+def emit(
+    block, grad_tok, weights, filters,
+    block_out, grad_out, out_q, out_v, out_o, out_f,
+    wide_w, wide_f, sem,
+):
+    copies = []
+
+    def leave(src, dst):
+        copy = pltpu.make_async_copy(src, dst, sem.at[len(copies)])
+        copy.start()
+        copies.append(copy)
+
+    leave(block, block_out)
+    leave(grad_tok, grad_out)
+    wide_f[...] = filters[...].reshape(wide_f.shape).astype(wide_f.dtype)
+    leave(wide_f, out_f)
+    for m, dst in enumerate((out_q, out_o, out_v)):
+        wide_w[m] = weights[m].reshape(dst.shape).astype(wide_w.dtype)
+        leave(wide_w.at[m], dst)
+    for copy in copies:
+        copy.wait()
 
 
 def short_body(tokens, w_query, w_value, w_out, long_filter, cotangent):
@@ -604,17 +607,14 @@
     block, grad_tok, weights, filters = pl.pallas_call(
         functools.partial(fused, scale),
         out_shape=(
-            jax.ShapeDtypeStruct((here, 2 * half), b16),
-            jax.ShapeDtypeStruct((here, 2 * half), b16),
-            jax.ShapeDtypeStruct((3, batches, quarter, half), b16),
-            jax.ShapeDtypeStruct((batches, quarter, length), b16),
+            vmem((here, 2 * half), b16),
+            vmem((here, 2 * half), b16),
+            vmem((3, batches, quarter, half), b16),
+            vmem((batches, quarter, length), b16),
         ),
         in_specs=[pl.BlockSpec(memory_space=pltpu.HBM)] * 8,
-        out_specs=(pl.BlockSpec(memory_space=pltpu.HBM),) * 4,
+        out_specs=(pl.BlockSpec(memory_space=pltpu.VMEM),) * 4,
         scratch_shapes=[
-            vmem((here, 2 * half), b16),
-            vmem((here, 2 * half), b16),
-            dma((6,)),
             *(vmem(a.shape, a.dtype) for a in arguments),
             dma((8,)),
             vmem((length, 2 * length), b16),
@@ -649,7 +649,6 @@
             vmem((3, 3, levels, quarter, half), b16),
             vmem((3, levels, quarter, half), b16),
             vmem((3, levels, quarter, half), b16),
-            vmem((3, batches, quarter, half), b16),
             vmem((2, own, length), f32),
             vmem((2, 2 * quarter, length), f32),
             vmem((2, quarter, length), f32),
@@ -659,7 +658,6 @@
             vmem((2, quarter, length), b16),
             vmem((quarter, length), b16),
             vmem((quarter, length), b16),
-            vmem((batches, quarter, length), b16),
             dma((4,)),
             dma((4,)),
             dma((4, 3)),
@@ -684,8 +682,9 @@
             jax.ShapeDtypeStruct((own, length), f32),
         ),
         in_specs=[pl.BlockSpec(memory_space=pltpu.VMEM)] * 4,
-        out_specs=(pl.BlockSpec(memory_space=pltpu.VMEM),) * 6,
-        compiler_params=pltpu.CompilerParams(vmem_limit_bytes=65900000),
+        out_specs=(pl.BlockSpec(memory_space=pltpu.HBM),) * 6,
+        scratch_shapes=[vmem((3, own, half), f32), vmem((own, length), f32), dma((6,))],
+        compiler_params=pltpu.CompilerParams(vmem_limit_bytes=8000000),
     )(block, grad_tok, weights, filters)
     return (block[None], grad_tok[None], *sums)
 

time: 48.5 us -> 46.7 us (0.963)
  Pallas kernels: 47.7 us -> 45.9 us
    pallas_call x1, Pallas kernels: 2.15 us -> 1.06 us  [short_body(): pl.pallas_call(emit, out_shape=(jax.ShapeDtypeStruct((here, 2 * half), b1...]
    pallas_call x1, Pallas kernels: 45.6 us -> 44.9 us  [short_body(): pl.pallas_call(functools.partial(fused, scale), out_shape=(vmem((here, 2...]
where the time goes in v3:
time: 46.7 us; the launch traced here: 46.6 us
  Pallas kernels  45.9 us (98%)
  between operations  0.64 us (1%)
    pallas_call x1, Pallas kernels, short_body(): pl.pallas_call(functools.partial(fused, scale), out_shape=(vmem((here, 2...  44.9 us
    pallas_call x1, Pallas kernels, short_body(): pl.pallas_call(emit, out_shape=(jax.ShapeDtypeStruct((here, 2 * half), b1...  1.06 us

profile of v3, /device:TPU:0, one launch (start us, length us, event | category | flops | bytes accessed | tf_op | source)
XLA Modules:
  0.0 46.6 jit_solution(9808228727497714308)
XLA Ops:
  0.6 44.9 %shard_map.127 = (bf16[128,1024]{1,0:T(8,128)(2,1)S(1)}, bf16[128,1024]{1,0:T(8,128)(2,1)S(1)}, bf16[3,4,16,512]{3,2,1,0:T(8,128)(2,1)S(1)}, bf16[4,16,1024]{2,1,0:T(8,128)(2,1)S(1)}) custom-call(bf16[128,1024]{1,0:T(8,128)(2,1)} %bitcast.4, bf16[512,512]{1,0:T(8,128)(2,1)} %wq_in.1, bf16[512,512]{1,0:T(8,128)(2,1)} %wv_in.1, bf16[512,512]{1,0:T(8,128)(2,1)} %wo_in.1, ...), custom_call_target="tpu_custom_call" | custom-call | tf_op jit(solution)/shard_map/pallas_call | solution.py:607
  45.5 1.1 %shard_map.128 = (bf16[128,1024]{1,0:T(8,128)(2,1)}, bf16[128,1024]{1,0:T(8,128)(2,1)}, f32[64,512]{1,0:T(8,128)}, f32[64,512]{1,0:T(8,128)}, f32[64,512]{1,0:T(8,128)}, /*index=5*/f32[64,1024]{1,0:T(8,128)}) custom-call(bf16[128,1024]{1,0:T(8,128)(2,1)S(1)} %get-tuple-element.16.block, bf16[128,1024]{1,0:T(8,128)(2,1)S(1)} %get-tuple-element.17.grad_tok, ...), custom_call_target="tpu_custom_call" | custom-call | tf_op jit(solution)/shard_map/pallas_call | solution.py:674

commit v4 on v3

--- a/solution.py
+++ b/solution.py
@@ -234,6 +234,7 @@
     both_taps, vspec, gspec, hspec, yspec, fspec,
     ssem1, rsem1, lsem1, ssem2, rsem2, lsem2, ssem_t, rsem_t,
     acc, kept, send_a, recv_a, send_b, recv_b, send_c, recv_c,
+    kept_z, send_z, recv_z, send_x, recv_x,
     acc_f, kept_f, last_f, send_af, recv_af, send_bf, recv_bf, send_cf, recv_cf,
     ssem_a, rsem_a, ssem_b, rsem_b, ssem_c, rsem_c, ssem_d, rsem_d,
 ):
@@ -482,6 +483,48 @@
             for r in range(1, batches)
         ]
 
+    def stage_bz(m, copy):
+        copy.wait()
+
+        def pick(z):
+            mine = acc[m, pl.ds(z, 1), :, part_of(low, 2 * quarter), :]
+            return (mine + recv_a[m, pl.ds(z, 1)].astype(f32)).reshape(2, 2 * quarter, half)
+
+        copies = []
+        for r in range(1, levels):
+            z = lax.rem(level + r, levels)
+            send_z[r - 1] = pick(z).astype(b16)
+            copies.append(
+                remote(
+                    send_z.at[r - 1], recv_z.at[r - 1], ssem_b.at[m, r - 1], rsem_b.at[m, r - 1],
+                    seq=2 * z + column,
+                )
+            )
+        kept_z[...] = pick(level)
+        return copies
+
+    def stage_cz(m, copies):
+        wait(copies)
+        kept_z[...] = kept_z[...] + jnp.sum(recv_z[...].astype(f32), axis=0)
+        copies = []
+        for index, (dx, dy) in enumerate(((1, 1), (1, 0), (0, 1))):
+            x = 1 - column if dx else column
+            y = 1 - high if dy else high
+            send_x[index] = kept_z[x, part_of(y, quarter), :].astype(b16)
+            copies.append(
+                remote(
+                    send_x.at[index], recv_x.at[index], ssem_c.at[m, index], rsem_c.at[m, index],
+                    seq=across if dx else me, batch=facing if dy else seat,
+                )
+            )
+        return copies
+
+    def stage_dz(m, copies):
+        wait(copies)
+        mine = kept_z[column, part_of(high, quarter), :]
+        out_w[m, slot] = (mine + jnp.sum(recv_x[...].astype(f32), axis=0)).astype(b16)
+        return share(m, out_w.at[m])
+
     def stage_d(m, copies):
         wait(copies)
         out_w[m, slot] = jnp.sum(recv_c[m].astype(f32), axis=0).astype(b16)
@@ -503,7 +546,6 @@
         signal(other, other), table_of(other)
     )
     full_v = returned(1, other, vspec[rows_at(other), :], False)
-
     wait(own_g)
     gspec[...] = matmul(own_signals(1), table_of(side))
     self_g = returned(2, 2 + other, gspec[rows_at(other), :], True)
@@ -533,11 +575,7 @@
     weight(1, matmul(gated.T, ups[...]))
     a1 = stage_a(1)
     b0 = stage_b(0, a0)
-    bf.wait()
-    last_f[...] = kept_f[:, part_of(high, quarter), :] + recv_bf[...].astype(f32)
-    send_cf[...] = last_f[other].astype(b16)
-    cf = remote(send_cf, recv_cf, ssem_c.at[3, 0], rsem_c.at[3, 0], seq=partner)
-    b1 = stage_b(1, a1)
+    b1 = stage_bz(1, a1)
     wait(self_g)
     wait(full_g)
     value_0, value_1 = rejoin(2), rejoin(3)
@@ -546,22 +584,27 @@
     a2 = stage_a(2)
     total = strands[...].astype(f32) + matmul(gated, wo[...])
     block_out[:, :half] = total[:here].astype(b16)
+    last = total[here:].astype(b16)
     b2 = stage_b(2, a2)
-    block_out[:, half:] = matmul(total[here:].astype(b16), flip).astype(b16)
+    bf.wait()
+    last_f[...] = kept_f[:, part_of(high, quarter), :] + recv_bf[...].astype(f32)
+    send_cf[...] = last_f[other].astype(b16)
+    cf = remote(send_cf, recv_cf, ssem_c.at[3, 0], rsem_c.at[3, 0], seq=partner)
+    block_out[:, half:] = matmul(last, flip).astype(b16)
     c0 = stage_c(0, b0)
-    cf.wait()
-    out_f[slot] = (last_f[side] + recv_cf[...].astype(f32)).astype(b16)
-    df = share(3, out_f)
-    c1 = stage_c(1, b1)
+    c1 = stage_cz(1, b1)
     total = ups[...].astype(f32) + matmul_t(grad_query, wq[...]) + matmul_t(grad_value, wv[...])
     grad_out[:, :half] = total[:here].astype(b16)
     grad_out[:, half:] = matmul(total[here:].astype(b16), flip).astype(b16)
     d0 = stage_d(0, c0)
     c2 = stage_c(2, b2)
-    d1 = stage_d(1, c1)
-    wait(df)
+    cf.wait()
+    out_f[slot] = (last_f[side] + recv_cf[...].astype(f32)).astype(b16)
+    df = share(3, out_f)
+    d1 = stage_dz(1, c1)
     wait(d0)
     d2 = stage_d(2, c2)
+    wait(df)
     wait(d1)
     wait(d2)
 
@@ -649,6 +692,11 @@
             vmem((3, 3, levels, quarter, half), b16),
             vmem((3, levels, quarter, half), b16),
             vmem((3, levels, quarter, half), b16),
+            vmem((2, 2 * quarter, half), f32),
+            vmem((3, 2, 2 * quarter, half), b16),
+            vmem((3, 2, 2 * quarter, half), b16),
+            vmem((3, quarter, half), b16),
+            vmem((3, quarter, half), b16),
             vmem((2, own, length), f32),
             vmem((2, 2 * quarter, length), f32),
             vmem((2, quarter, length), f32),

time: 46.7 us -> 46.1 us (0.987)
  Pallas kernels: 45.9 us -> 45.3 us
    pallas_call x1, Pallas kernels: 44.9 us -> 44.2 us  [short_body(): pl.pallas_call(functools.partial(fused, scale), out_shape=(vmem((here, 2...]
where the time goes in v4:
time: 46.1 us; the launch traced here: 45.9 us
  Pallas kernels  45.3 us (98%)
  between operations  0.64 us (1%)
    pallas_call x1, Pallas kernels, short_body(): pl.pallas_call(functools.partial(fused, scale), out_shape=(vmem((here, 2...  44.2 us
    pallas_call x1, Pallas kernels, short_body(): pl.pallas_call(emit, out_shape=(jax.ShapeDtypeStruct((here, 2 * half), b1...  1.06 us

profile of v4, /device:TPU:0, one launch (start us, length us, event | category | flops | bytes accessed | tf_op | source)
XLA Modules:
  0.0 45.9 jit_solution(6698749970035735782)
XLA Ops:
  0.6 44.2 %shard_map.127 = (bf16[128,1024]{1,0:T(8,128)(2,1)S(1)}, bf16[128,1024]{1,0:T(8,128)(2,1)S(1)}, bf16[3,4,16,512]{3,2,1,0:T(8,128)(2,1)S(1)}, bf16[4,16,1024]{2,1,0:T(8,128)(2,1)S(1)}) custom-call(bf16[128,1024]{1,0:T(8,128)(2,1)} %bitcast.4, bf16[512,512]{1,0:T(8,128)(2,1)} %wq_in.1, bf16[512,512]{1,0:T(8,128)(2,1)} %wv_in.1, bf16[512,512]{1,0:T(8,128)(2,1)} %wo_in.1, ...), custom_call_target="tpu_custom_call" | custom-call | tf_op jit(solution)/shard_map/pallas_call | solution.py:650
  44.8 1.1 %shard_map.128 = (bf16[128,1024]{1,0:T(8,128)(2,1)}, bf16[128,1024]{1,0:T(8,128)(2,1)}, f32[64,512]{1,0:T(8,128)}, f32[64,512]{1,0:T(8,128)}, f32[64,512]{1,0:T(8,128)}, /*index=5*/f32[64,1024]{1,0:T(8,128)}) custom-call(bf16[128,1024]{1,0:T(8,128)(2,1)S(1)} %get-tuple-element.16.block, bf16[128,1024]{1,0:T(8,128)(2,1)S(1)} %get-tuple-element.17.grad_tok, ...), custom_call_target="tpu_custom_call" | custom-call | tf_op jit(solution)/shard_map/pallas_call | solution.py:722

commit v5 on v4

--- a/solution.py
+++ b/solution.py
@@ -556,15 +556,9 @@
     acc_f[...] = (matmul_t(fspec[...], table[...]) * (scale / length)).reshape(2, own, length)
     send_af[...] = acc_f[:, part_of(1 - low, 2 * quarter), :].astype(b16)
     af = remote(send_af, recv_af, ssem_a.at[3], rsem_a.at[3], batch=2 * high + 1 - low)
-    af.wait()
-    kept_f[...] = acc_f[:, part_of(low, 2 * quarter), :] + recv_af[...].astype(f32)
-    send_bf[...] = kept_f[:, part_of(1 - high, quarter), :].astype(b16)
-    bf = remote(send_bf, recv_bf, ssem_b.at[3, 0], rsem_b.at[3, 0], batch=facing)
     wait(cross_g)
-    gspec[rows_at(side), :] = gspec[rows_at(side), :] + matmul(
-        signal(2 + side, other), table_of(other)
-    )
-    full_g = returned(3, 2 + side, gspec[rows_at(side), :], False)
+    whole = gspec[rows_at(side), :] + matmul(signal(2 + side, other), table_of(other))
+    full_g = returned(3, 2 + side, whole, False)
     wait(self_v)
     wait(full_v)
     conv = jnp.concatenate([rejoin(0), rejoin(1)], axis=0).astype(f32)
@@ -576,6 +570,10 @@
     a1 = stage_a(1)
     b0 = stage_b(0, a0)
     b1 = stage_bz(1, a1)
+    af.wait()
+    kept_f[...] = acc_f[:, part_of(low, 2 * quarter), :] + recv_af[...].astype(f32)
+    send_bf[...] = kept_f[:, part_of(1 - high, quarter), :].astype(b16)
+    bf = remote(send_bf, recv_bf, ssem_b.at[3, 0], rsem_b.at[3, 0], batch=facing)
     wait(self_g)
     wait(full_g)
     value_0, value_1 = rejoin(2), rejoin(3)
@@ -586,26 +584,26 @@
     block_out[:, :half] = total[:here].astype(b16)
     last = total[here:].astype(b16)
     b2 = stage_b(2, a2)
+    block_out[:, half:] = matmul(last, flip).astype(b16)
+    c0 = stage_c(0, b0)
+    c1 = stage_cz(1, b1)
     bf.wait()
     last_f[...] = kept_f[:, part_of(high, quarter), :] + recv_bf[...].astype(f32)
     send_cf[...] = last_f[other].astype(b16)
     cf = remote(send_cf, recv_cf, ssem_c.at[3, 0], rsem_c.at[3, 0], seq=partner)
-    block_out[:, half:] = matmul(last, flip).astype(b16)
-    c0 = stage_c(0, b0)
-    c1 = stage_cz(1, b1)
     total = ups[...].astype(f32) + matmul_t(grad_query, wq[...]) + matmul_t(grad_value, wv[...])
     grad_out[:, :half] = total[:here].astype(b16)
     grad_out[:, half:] = matmul(total[here:].astype(b16), flip).astype(b16)
     d0 = stage_d(0, c0)
     c2 = stage_c(2, b2)
+    d1 = stage_dz(1, c1)
     cf.wait()
     out_f[slot] = (last_f[side] + recv_cf[...].astype(f32)).astype(b16)
     df = share(3, out_f)
-    d1 = stage_dz(1, c1)
     wait(d0)
     d2 = stage_d(2, c2)
+    wait(d1)
     wait(df)
-    wait(d1)
     wait(d2)
 
 

time: 46.1 us -> 45.5 us (0.987)
  Pallas kernels: 45.3 us -> 44.8 us
    pallas_call x1, Pallas kernels: 44.2 us -> 43.7 us  [short_body(): pl.pallas_call(functools.partial(fused, scale), out_shape=(vmem((here, 2...]
where the time goes in v5:
time: 45.5 us; the launch traced here: 45.4 us
  Pallas kernels  44.8 us (98%)
  between operations  0.64 us (1%)
    pallas_call x1, Pallas kernels, short_body(): pl.pallas_call(functools.partial(fused, scale), out_shape=(vmem((here, 2...  43.7 us
    pallas_call x1, Pallas kernels, short_body(): pl.pallas_call(emit, out_shape=(jax.ShapeDtypeStruct((here, 2 * half), b1...  1.06 us

profile of v5, /device:TPU:0, one launch (start us, length us, event | category | flops | bytes accessed | tf_op | source)
XLA Modules:
  0.0 45.4 jit_solution(17360382463564597986)
XLA Ops:
  0.6 43.7 %shard_map.127 = (bf16[128,1024]{1,0:T(8,128)(2,1)S(1)}, bf16[128,1024]{1,0:T(8,128)(2,1)S(1)}, bf16[3,4,16,512]{3,2,1,0:T(8,128)(2,1)S(1)}, bf16[4,16,1024]{2,1,0:T(8,128)(2,1)S(1)}) custom-call(bf16[128,1024]{1,0:T(8,128)(2,1)} %bitcast.4, bf16[512,512]{1,0:T(8,128)(2,1)} %wq_in.1, bf16[512,512]{1,0:T(8,128)(2,1)} %wv_in.1, bf16[512,512]{1,0:T(8,128)(2,1)} %wo_in.1, ...), custom_call_target="tpu_custom_call" | custom-call | tf_op jit(solution)/shard_map/pallas_call | solution.py:648
  44.3 1.1 %shard_map.128 = (bf16[128,1024]{1,0:T(8,128)(2,1)}, bf16[128,1024]{1,0:T(8,128)(2,1)}, f32[64,512]{1,0:T(8,128)}, f32[64,512]{1,0:T(8,128)}, f32[64,512]{1,0:T(8,128)}, /*index=5*/f32[64,1024]{1,0:T(8,128)}) custom-call(bf16[128,1024]{1,0:T(8,128)(2,1)S(1)} %get-tuple-element.16.block, bf16[128,1024]{1,0:T(8,128)(2,1)S(1)} %get-tuple-element.17.grad_tok, ...), custom_call_target="tpu_custom_call" | custom-call | tf_op jit(solution)/shard_map/pallas_call | solution.py:720

commit v6 on v5

--- a/solution.py
+++ b/solution.py
@@ -446,7 +446,7 @@
             return (mine + theirs).reshape(levels, quarter, half)
 
         copies = []
-        for index, (dx, dy) in enumerate(((1, 1), (1, 0), (0, 1))):
+        for index, (dx, dy) in enumerate(((0, 1), (1, 0), (1, 1))):
             x = 1 - column if dx else column
             y = 1 - high if dy else high
             send_b[m, index] = pick(x, y).astype(b16)
@@ -507,7 +507,7 @@
         wait(copies)
         kept_z[...] = kept_z[...] + jnp.sum(recv_z[...].astype(f32), axis=0)
         copies = []
-        for index, (dx, dy) in enumerate(((1, 1), (1, 0), (0, 1))):
+        for index, (dx, dy) in enumerate(((0, 1), (1, 0), (1, 1))):
             x = 1 - column if dx else column
             y = 1 - high if dy else high
             send_x[index] = kept_z[x, part_of(y, quarter), :].astype(b16)

time: 45.5 us -> 45.3 us (level)
  Pallas kernels: 44.8 us -> 44.3 us
    pallas_call x1, Pallas kernels: 43.7 us -> 43.2 us  [short_body(): pl.pallas_call(functools.partial(fused, scale), out_shape=(vmem((here, 2...]
where the time goes in v6:
time: 45.3 us; the launch traced here: 44.9 us
  Pallas kernels  44.3 us (98%)
  between operations  0.64 us (1%)
    pallas_call x1, Pallas kernels, short_body(): pl.pallas_call(functools.partial(fused, scale), out_shape=(vmem((here, 2...  43.2 us
    pallas_call x1, Pallas kernels, short_body(): pl.pallas_call(emit, out_shape=(jax.ShapeDtypeStruct((here, 2 * half), b1...  1.06 us

profile of v6, /device:TPU:0, one launch (start us, length us, event | category | flops | bytes accessed | tf_op | source)
XLA Modules:
  0.0 44.9 jit_solution(17301301120543471463)
XLA Ops:
  0.6 43.2 %shard_map.127 = (bf16[128,1024]{1,0:T(8,128)(2,1)S(1)}, bf16[128,1024]{1,0:T(8,128)(2,1)S(1)}, bf16[3,4,16,512]{3,2,1,0:T(8,128)(2,1)S(1)}, bf16[4,16,1024]{2,1,0:T(8,128)(2,1)S(1)}) custom-call(bf16[128,1024]{1,0:T(8,128)(2,1)} %bitcast.4, bf16[512,512]{1,0:T(8,128)(2,1)} %wq_in.1, bf16[512,512]{1,0:T(8,128)(2,1)} %wv_in.1, bf16[512,512]{1,0:T(8,128)(2,1)} %wo_in.1, ...), custom_call_target="tpu_custom_call" | custom-call | tf_op jit(solution)/shard_map/pallas_call | solution.py:648
  43.9 1.1 %shard_map.128 = (bf16[128,1024]{1,0:T(8,128)(2,1)}, bf16[128,1024]{1,0:T(8,128)(2,1)}, f32[64,512]{1,0:T(8,128)}, f32[64,512]{1,0:T(8,128)}, f32[64,512]{1,0:T(8,128)}, /*index=5*/f32[64,1024]{1,0:T(8,128)}) custom-call(bf16[128,1024]{1,0:T(8,128)(2,1)S(1)} %get-tuple-element.16.block, bf16[128,1024]{1,0:T(8,128)(2,1)S(1)} %get-tuple-element.17.grad_tok, ...), custom_call_target="tpu_custom_call" | custom-call | tf_op jit(solution)/shard_map/pallas_call | solution.py:720
